TPU v7x, 256 devices: a whole 4x4x8 slice. The times are simulated.
256 devices in a mesh: row: 32 (over x_lo, z, core), col: 8 (over y, x_hi).
Axes of the slice: x: 4 (x_hi: 2, x_lo: 2; x = x_hi * 2 + x_lo), y: 4, z: 8, core: 2. Of those that a mesh axis runs over, the one named last changes fastest.
Arguments:
- maps: bfloat16 [48, 1024, 1024], P(None, 'row', 'col'), may hold values from -6 to 6
- kernel: bfloat16 [3, 3, 48, 48], replicated, may hold values from -0.3125 to 0.3125
- mixing: bfloat16 [48, 48], replicated, may hold values from -0.875 to 0.875
- cotangent: bfloat16 [48, 1024, 1024], P(None, 'row', 'col'), may hold values from -6 to 6
Outputs:
- output: bfloat16 [48, 1024, 1024], P(None, 'row', 'col')
- grad_maps: bfloat16 [48, 1024, 1024], P(None, 'row', 'col')
- grad_kernel: float32 [3, 3, 48, 48], replicated
- grad_mixing: float32 [48, 48], replicated
All inputs are finite; a program needn't handle non-finite values.
Results may differ from a plain program's by a relative error of at most 0.0056.
Values may be sent and summed in bfloat16 or wider, within the bound.
A program may use at most 128 MiB of HBM per device.

v0:
```python
import functools

import jax
import jax.numpy as jnp
from jax import lax
from jax.experimental import pallas as pl
from jax.experimental.pallas import tpu as pltpu
from jax.sharding import PartitionSpec as P

DILATION = 8


def with_halo(array, sides, width):
    for axis, dim in sides:
        peers, length = (lax.axis_size(axis), array.shape[dim])
        up = [(i, (i + 1) % peers) for i in range(peers - 1)]
        down = [(j, i) for i, j in up]
        last = lax.slice_in_dim(array, length - width, length, axis=dim)
        initial = lax.slice_in_dim(array, 0, width, axis=dim)
        before = lax.ppermute(last, axis, up)
        after = lax.ppermute(initial, axis, down)
        array = jnp.concatenate([before, array, after], axis=dim)
    return array


def flip(index, stride):
    return index + stride - 2 * stride * ((index // stride) % 2)


def sum_kernel(strides, x_ref, out_ref, arrived, partial, send_sem, recv_sem):
    row, col = lax.axis_index("row"), lax.axis_index("col")
    partners = [(flip(row, stride), col) if axis == "row" else (row, flip(col, stride)) for axis, stride in strides]
    barrier = pltpu.get_barrier_semaphore()
    for partner in partners:
        pl.semaphore_signal(barrier, inc=1, device_id=partner, device_id_type=pl.DeviceIdType.MESH)
    pl.semaphore_wait(barrier, len(partners))
    source = x_ref
    for step, partner in enumerate(partners):
        copy = pltpu.make_async_remote_copy(
            src_ref=source,
            dst_ref=arrived.at[step],
            send_sem=send_sem.at[step],
            recv_sem=recv_sem.at[step],
            device_id=partner,
            device_id_type=pl.DeviceIdType.MESH,
        )
        copy.start()
        copy.wait()
        target = out_ref if step == len(partners) - 1 else partial.at[step]
        target[...] = source[...] + arrived[step]
        source = target


def all_sum(x):
    strides = []
    for axis in ("row", "col"):
        peers = lax.axis_size(axis)
        stride = 1
        while stride < peers:
            strides.append((axis, stride))
            stride *= 2
    count = len(strides)
    return pl.pallas_call(
        functools.partial(sum_kernel, strides),
        out_shape=jax.ShapeDtypeStruct(x.shape, x.dtype),
        in_specs=[pl.BlockSpec(memory_space=pltpu.VMEM)],
        out_specs=pl.BlockSpec(memory_space=pltpu.VMEM),
        scratch_shapes=[
            pltpu.VMEM((count,) + x.shape, x.dtype),
            pltpu.VMEM((count,) + x.shape, x.dtype),
            pltpu.SemaphoreType.DMA((count,)),
            pltpu.SemaphoreType.DMA((count,)),
        ],
        compiler_params=pltpu.CompilerParams(collective_id=0, has_side_effects=True),
    )(x)


def mirror_tile(tile):
    row_count = lax.axis_size("row")
    col_count = lax.axis_size("col")
    chans, rows, cols = tile.shape
    group = cols // rows
    turn = lax.axis_index("row") % group
    pieces = jnp.roll(tile.reshape(chans, rows, group, rows), -turn, axis=2)
    landed = []
    for k in range(group):
        piece = jnp.swapaxes(pieces[:, :, k, :], 1, 2).reshape(chans, rows * rows)
        pairs = []
        for source_row in range(row_count):
            for source_col in range(col_count):
                target_row = group * source_col + (source_row % group + k) % group
                target = target_row * col_count + source_row // group
                pairs.append((source_row * col_count + source_col, target))
        landed.append(lax.ppermute(piece, ("row", "col"), pairs).reshape(chans, rows, rows))
    slots = jnp.stack([landed[(-i) % group] for i in range(group)], axis=2)
    return jnp.roll(slots, turn, axis=2).reshape(chans, rows, cols)


def window(padded, top, left, rows, cols):
    return padded[:, top : top + rows, left : left + cols]


def shards(maps, kernel, mixing, cotangent):
    chans, rows, cols = maps.shape
    map_bins = rows * lax.axis_size("row")
    active = jnp.maximum(maps, 0)
    padded = with_halo(active, (("row", 1), ("col", 2)), DILATION)
    before = jnp.zeros((chans, rows, cols), jnp.float32)
    for row_tap in range(3):
        for col_tap in range(3):
            piece = window(padded, DILATION * row_tap, DILATION * col_tap, rows, cols)
            before = before + jnp.einsum(
                "io,ihw->ohw", kernel[row_tap, col_tap], piece, preferred_element_type=jnp.float32
            )
    hidden = jnp.maximum(before, 0.0).astype(jnp.bfloat16)
    mixed = jnp.einsum("io,ihw->ohw", mixing, hidden, preferred_element_type=jnp.float32).astype(
        jnp.bfloat16
    )
    mixed_turned = mirror_tile(mixed)
    grad_turned = mirror_tile(cotangent)
    output = (
        maps.astype(jnp.float32)
        + 0.5 * (mixed.astype(jnp.float32) + mixed_turned.astype(jnp.float32))
    ).astype(jnp.bfloat16)
    grad_wide = cotangent.astype(jnp.float32)
    grad_mixed = (0.5 * (grad_wide + grad_turned.astype(jnp.float32))).astype(jnp.bfloat16)
    local_mixing = jnp.einsum("ihw,ohw->io", hidden, grad_mixed, preferred_element_type=jnp.float32)
    grad_hidden = jnp.einsum("io,ohw->ihw", mixing, grad_mixed, preferred_element_type=jnp.float32)
    grad_before = jnp.where(hidden > 0, grad_hidden, 0.0).astype(jnp.bfloat16)
    tap_grads = []
    for row_tap in range(3):
        for col_tap in range(3):
            piece = window(padded, DILATION * row_tap, DILATION * col_tap, rows, cols)
            tap_grads.append(
                jnp.einsum("ihw,ohw->io", piece, grad_before, preferred_element_type=jnp.float32)
            )
    local_kernel = jnp.stack(tap_grads).reshape(3, 3, chans, chans)
    flat = jnp.concatenate([local_kernel.reshape(-1), local_mixing.reshape(-1)])
    sums = all_sum(flat.reshape(-1, 128)).reshape(-1)
    grad_kernel = sums[: 9 * chans * chans].reshape(3, 3, chans, chans)
    grad_mixing = sums[9 * chans * chans :].reshape(chans, chans)
    grad_padded = with_halo(grad_before, (("row", 1), ("col", 2)), DILATION)
    grad_active = jnp.zeros((chans, rows, cols), jnp.float32)
    for row_tap in range(3):
        for col_tap in range(3):
            piece = window(
                grad_padded,
                2 * DILATION - DILATION * row_tap,
                2 * DILATION - DILATION * col_tap,
                rows,
                cols,
            )
            grad_active = grad_active + jnp.einsum(
                "io,ohw->ihw", kernel[row_tap, col_tap], piece, preferred_element_type=jnp.float32
            )
    grad_maps = (grad_wide + jnp.where(maps > 0, grad_active, 0.0)).astype(jnp.bfloat16)
    return (output, grad_maps, grad_kernel / map_bins, grad_mixing / map_bins)


def solution(mesh):
    placed = (P(None, "row", "col"), P(), P(), P(None, "row", "col"))
    return jax.shard_map(
        shards,
        mesh=mesh,
        in_specs=placed,
        out_specs=(P(None, "row", "col"), P(None, "row", "col"), P(), P()),
        check_vma=False,
    )
```

profile of v0, /device:TPU:6, one launch (start us, length us, event | category | flops | bytes accessed | tf_op | source)
XLA Modules:
  0.0 197.2 jit_solution(6545544361003452266)
XLA Ops:
  0.7 1.2 copy_maximum_fusion
  1.9 1.9 collective-permute-start
  3.8 7.5 %collective-permute-start.1 = (bf16[48,8,128]{2,0,1:T(8,128)(2,1)S(1)}, bf16[48,8,128]{2,0,1:T(8,128)(2,1)S(1)}, u32[]{:S(2)}, u32[]{:S(2)}) collective-permute-start(bf16[48,8,128]{2,0,1:T(8,128)(2,1)S(1)} %get-tuple-element.40), channel_id=1, source_target_pairs={{8,0},{16,8},{24,16},{32,24},{40,32},{48,40},{56,48},{64,56},{72,6... | collective-permute-start | bytes 294920 | tf_op jit(solution)/shard_map/ppermute | solution.py:21
  11.3 0.6 copy.147
  12.0 0.5 fusion.29
  12.6 0.7 copy.151
  13.7 2.0 collective-permute-start.11
  15.7 0.7 copy.150
  16.8 3.1 %collective-permute-start.10 = (bf16[48,1024]{1,0:T(8,128)(2,1)S(1)}, bf16[48,1024]{1,0:T(8,128)(2,1)S(1)}, u32[]{:S(2)}, u32[]{:S(2)}) collective-permute-start(bf16[48,1024]{1,0:T(8,128)(2,1)S(1)} %reshape.69), channel_id=1, source_target_pairs={{0,16},{1,48},{2,80},{3,112},{4,144},{5,176},{6,208},{7,240},{8,24... | collective-permute-start | bytes 294920 | tf_op jit(solution)/shard_map/ppermute | solution.py:94
  19.9 0.7 copy.149
  20.6 1.0 reshape.68
  21.6 6.3 %collective-permute-start.9 = (bf16[48,1024]{1,0:T(8,128)(2,1)}, bf16[48,1024]{1,0:T(8,128)(2,1)S(1)}, u32[]{:S(2)}, u32[]{:S(2)}) collective-permute-start(bf16[48,1024]{1,0:T(8,128)(2,1)} %reshape.68), channel_id=1, source_target_pairs={{0,24},{1,56},{2,88},{3,120},{4,152},{5,184},{6,216},{7,248},{8,0}... | collective-permute-start | bytes 294920 | tf_op jit(solution)/shard_map/ppermute | solution.py:94
  27.9 0.7 copy.148
  29.3 0.5 copy.121
  30.4 1.9 collective-permute-start.3
  32.3 6.3 %collective-permute-start.2 = (bf16[48,48,8]{1,2,0:T(8,128)(2,1)S(1)}, bf16[48,48,8]{1,2,0:T(8,128)(2,1)S(1)}, u32[]{:S(2)}, u32[]{:S(2)}) collective-permute-start(bf16[48,48,8]{1,2,0:T(8,128)(2,1)S(1)} %copy.121), channel_id=1, source_target_pairs={{0,1},{1,2},{2,3},{3,4},{4,5},{5,6},{6,7},{8,9},{9,10},{10,11},{11... | collective-permute-start | bytes 110600 | tf_op jit(solution)/shard_map/ppermute | solution.py:20
  38.9 1.9 collective-permute-done.2
  40.8 7.8 %collective-permute-start.8 = (bf16[48,1024]{1,0:T(8,128)(2,1)S(1)}, bf16[48,1024]{1,0:T(8,128)(2,1)S(1)}, u32[]{:S(2)}, u32[]{:S(2)}) collective-permute-start(bf16[48,1024]{1,0:T(8,128)(2,1)S(1)} %reshape.67), channel_id=1, source_target_pairs={{0,0},{1,32},{2,64},{3,96},{4,128},{5,160},{6,192},{7,224},{8,8},{... | collective-permute-start | bytes 294920 | tf_op jit(solution)/shard_map/ppermute | solution.py:94
  49.1 1.4 copy.126
  50.5 0.8 maximum_maximum_fusion
  52.6 0.7 copy-done.4
  54.2 1.0 fusion.11
  55.3 1.3 fusion.12
  57.1 0.5 fusion.37
  57.7 0.7 copy.139
  58.9 0.7 copy.138
  60.1 0.7 copy.137
  61.2 0.7 copy.136
  62.3 5.3 %collective-permute-start.6 = (bf16[48,1024]{1,0:T(8,128)(2,1)S(1)}, bf16[48,1024]{1,0:T(8,128)(2,1)S(1)}, u32[]{:S(2)}, u32[]{:S(2)}) collective-permute-start(bf16[48,1024]{1,0:T(8,128)(2,1)S(1)} %reshape.64), channel_id=1, source_target_pairs={{0,16},{1,48},{2,80},{3,112},{4,144},{5,176},{6,208},{7,240},{8,24... | collective-permute-start | bytes 294920 | tf_op jit(solution)/shard_map/ppermute | solution.py:94
  67.7 3.2 %collective-permute-start.5 = (bf16[48,1024]{1,0:T(8,128)(2,1)S(1)}, bf16[48,1024]{1,0:T(8,128)(2,1)S(1)}, u32[]{:S(2)}, u32[]{:S(2)}) collective-permute-start(bf16[48,1024]{1,0:T(8,128)(2,1)S(1)} %reshape.63), channel_id=1, source_target_pairs={{0,24},{1,56},{2,88},{3,120},{4,152},{5,184},{6,216},{7,248},{8,0}... | collective-permute-start | bytes 294920 | tf_op jit(solution)/shard_map/ppermute | solution.py:94
  70.9 6.1 %collective-permute-start.4 = (bf16[48,1024]{1,0:T(8,128)(2,1)S(1)}, bf16[48,1024]{1,0:T(8,128)(2,1)S(1)}, u32[]{:S(2)}, u32[]{:S(2)}) collective-permute-start(bf16[48,1024]{1,0:T(8,128)(2,1)S(1)} %reshape.62), channel_id=1, source_target_pairs={{0,0},{1,32},{2,64},{3,96},{4,128},{5,160},{6,192},{7,224},{8,8},{... | collective-permute-start | bytes 294920 | tf_op jit(solution)/shard_map/ppermute | solution.py:94
  78.1 18.9 %collective-permute-done.5 = bf16[48,1024]{1,0:T(8,128)(2,1)S(1)} collective-permute-done((bf16[48,1024]{1,0:T(8,128)(2,1)S(1)}, bf16[48,1024]{1,0:T(8,128)(2,1)S(1)}, u32[]{:S(2)}, u32[]{:S(2)}) %collective-permute-start.5) | collective-permute-done | bytes 98336 | tf_op jit(solution)/shard_map/ppermute | solution.py:94
  97.2 2.1 %collective-permute-done.4 = bf16[48,1024]{1,0:T(8,128)(2,1)S(1)} collective-permute-done((bf16[48,1024]{1,0:T(8,128)(2,1)S(1)}, bf16[48,1024]{1,0:T(8,128)(2,1)S(1)}, u32[]{:S(2)}, u32[]{:S(2)}) %collective-permute-start.4) | collective-permute-done | bytes 98336 | tf_op jit(solution)/shard_map/ppermute | solution.py:94
  99.5 4.5 %fusion.25 = (bf16[48,32,4,32]{0,3,2,1:T(8,128)(2,1)S(1)}, bf16[48,32,4,32]{0,3,2,1:T(8,128)(2,1)}) fusion(s32[]{:T(128)S(6)} %select_n.37, bf16[48,32,1,32]{0,3,2,1:T(8,128)(2,1)S(1)} %bitcast.228, bf16[48,32,1,32]{0,3,2,1:T(8,128)(2,1)S(1)} %bitcast.227, bf16[48,32,1,32]{0,3,2,1:T(8,128)(2,1)S(1)} %bitcast.226, bf16[48,32,1,32]{0,3,2,1:T(8,128)(2,1)S(1)} %bitcast.225, ...), kind=kLoop, calls=%fused_computation.74 | loop fusion | flops 2752512 | bytes 1572868 | tf_op jit(solution)/shard_map/jit(_roll_dynamic)/concatenate | solution.py:96
  104.3 0.6 copy.156
  104.9 1.6 convolution_bitcast_fusion.3
  106.5 1.3 fusion.8
  107.9 0.7 fusion.129
  108.5 1.2 fusion.21
  109.9 3.2 %collective-permute-start.12 = (bf16[48,8,128]{2,0,1:T(8,128)(2,1)}, bf16[48,8,128]{2,0,1:T(8,128)(2,1)}, u32[]{:S(2)}, u32[]{:S(2)}) collective-permute-start(bf16[48,8,128]{2,0,1:T(8,128)(2,1)} %get-tuple-element.37), channel_id=1, source_target_pairs={{0,8},{8,16},{16,24},{24,32},{32,40},{40,48},{48,56},{56,64},{64,7... | collective-permute-start | bytes 294920 | tf_op jit(solution)/shard_map/ppermute | solution.py:20
  113.1 4.7 %collective-permute-start.13 = (bf16[48,8,128]{2,0,1:T(8,128)(2,1)}, bf16[48,8,128]{2,0,1:T(8,128)(2,1)}, u32[]{:S(2)}, u32[]{:S(2)}) collective-permute-start(bf16[48,8,128]{2,0,1:T(8,128)(2,1)} %get-tuple-element.38), channel_id=1, source_target_pairs={{8,0},{16,8},{24,16},{32,24},{40,32},{48,40},{56,48},{64,56},{72,6... | collective-permute-start | bytes 294920 | tf_op jit(solution)/shard_map/ppermute | solution.py:21
  120.2 0.6 maximum_bitcast_fusion.x_ref
  120.9 45.5 %shard_map.75 = f32[180,128]{1,0:T(8,128)} custom-call(f32[180,128]{1,0:T(8,128)} %maximum_bitcast_fusion.x_ref), custom_call_target="tpu_custom_call" | custom-call | tf_op jit(solution)/shard_map/pallas_call | solution.py:63
  166.4 0.9 slice_multiply_fusion
  167.3 1.5 bitcast_convert_fusion.1
  168.8 1.5 copy.144
  170.2 1.4 add_convert_fusion
  171.6 0.7 slice_multiply_fusion.1
  172.3 0.7 div.21
  173.0 0.8 div.18
  173.8 0.8 copy.170
  174.7 1.0 pad_maximum_fusion.3
  175.9 0.5 copy.157
  177.0 1.9 collective-permute-start.15
  178.9 5.7 %collective-permute-start.14 = (bf16[48,48,8]{1,2,0:T(8,128)(2,1)S(1)}, bf16[48,48,8]{1,2,0:T(8,128)(2,1)S(1)}, u32[]{:S(2)}, u32[]{:S(2)}) collective-permute-start(bf16[48,48,8]{1,2,0:T(8,128)(2,1)S(1)} %copy.157), channel_id=1, source_target_pairs={{1,0},{2,1},{3,2},{4,3},{5,4},{6,5},{7,6},{9,8},{10,9},{11,10},{12... | collective-permute-start | bytes 110600 | tf_op jit(solution)/shard_map/ppermute | solution.py:21
  184.6 2.0 %fusion.46 = f32[32,128,48]{1,2,0:T(8,128)} fusion(bf16[48,8,128]{2,0,1:T(8,128)(2,1)} %collective-permute-done.13, bf16[48,32,128]{2,0,1:T(8,128)(2,1)S(1)} %fusion.8, bf16[3,3,48,48]{3,2,1,0:T(8,128)(2,1)S(1)} %copy-done.14), kind=kOutput, calls=%fused_computation.101 | convolution fusion | flops 19857408 | bytes 1290240 | tf_op jit(solution)/shard_map/io,ohw->ihw/dot_general | solution.py:153
  186.6 1.1 fusion.50
  187.8 1.3 copy.158
  189.1 1.3 copy.162
  190.4 2.1 %pad_maximum_fusion.1 = (bf16[48,48,136]{2,0,1:T(8,128)(2,1)S(1)}, bf16[48,48,136]{2,0,1:T(8,128)(2,1)S(1)}) fusion(bf16[48,48,8]{2,0,1:T(8,128)(2,1)} %copy.158, bf16[48,8,128]{2,0,1:T(8,128)(2,1)} %collective-permute-done.13, bf16[48,32,128]{2,0,1:T(8,128)(2,1)S(1)} %fusion.8, bf16[48,8,128]{2,0,1:T(8,128)(2,1)} %collective-permute-done.12, ...), kind=kLoop, calls=%fused_computation.50 | loop fusion | flops 5013504 | bytes 1916928 | tf_op jit(solution)/shard_map/concatenate | solution.py:22
  192.8 0.9 copy-done.12
  195.1 0.7 copy-done.3
  195.8 0.6 fusion.9
  196.4 0.8 copy.171
  (91 shorter events, 13.8 us)
Async XLA Ops:
  0.6 54.7 %copy-start = (bf16[48,48]{1,0:T(8,128)(2,1)S(1)}, bf16[48,48]{1,0:T(8,128)(2,1)}, u32[]{:S(2)}) copy-start(bf16[48,48]{1,0:T(8,128)(2,1)} %param.8) | copy-start | bytes 13828
  0.6 10.7 %copy-start.1 = (bf16[48,32,128]{2,1,0:T(8,128)(2,1)S(1)}, bf16[48,32,128]{2,1,0:T(8,128)(2,1)}, u32[]{:S(2)}) copy-start(bf16[48,32,128]{2,1,0:T(8,128)(2,1)} %param.9) | copy-start | bytes 1179652
  1.9 27.1 %collective-permute-start = (bf16[48,8,128]{2,0,1:T(8,128)(2,1)S(1)}, bf16[48,8,128]{2,0,1:T(8,128)(2,1)S(1)}, u32[]{:S(2)}, u32[]{:S(2)}) collective-permute-start(bf16[48,8,128]{2,0,1:T(8,128)(2,1)S(1)} %get-tuple-element.39), channel_id=1, source_target_pairs={{0,8},{8,16},{16,24},{24,32},{32,40},{40,48},{48,56},{56,64},{64,7... | collective-permute-start | bytes 294920 | tf_op jit(solution)/shard_map/ppermute | solution.py:20
  3.8 25.2 %collective-permute-start.1 = (bf16[48,8,128]{2,0,1:T(8,128)(2,1)S(1)}, bf16[48,8,128]{2,0,1:T(8,128)(2,1)S(1)}, u32[]{:S(2)}, u32[]{:S(2)}) collective-permute-start(bf16[48,8,128]{2,0,1:T(8,128)(2,1)S(1)} %get-tuple-element.40), channel_id=1, source_target_pairs={{8,0},{16,8},{24,16},{32,24},{40,32},{48,40},{56,48},{64,56},{72,6... | collective-permute-start | bytes 294920 | tf_op jit(solution)/shard_map/ppermute | solution.py:21
  13.7 48.6 %collective-permute-start.11 = (bf16[48,1024]{1,0:T(8,128)(2,1)S(1)}, bf16[48,1024]{1,0:T(8,128)(2,1)S(1)}, u32[]{:S(2)}, u32[]{:S(2)}) collective-permute-start(bf16[48,1024]{1,0:T(8,128)(2,1)S(1)} %reshape.70), channel_id=1, source_target_pairs={{0,8},{1,40},{2,72},{3,104},{4,136},{5,168},{6,200},{7,232},{8,16}... | collective-permute-start | bytes 294920 | tf_op jit(solution)/shard_map/ppermute | solution.py:94
  16.8 50.9 %collective-permute-start.10 = (bf16[48,1024]{1,0:T(8,128)(2,1)S(1)}, bf16[48,1024]{1,0:T(8,128)(2,1)S(1)}, u32[]{:S(2)}, u32[]{:S(2)}) collective-permute-start(bf16[48,1024]{1,0:T(8,128)(2,1)S(1)} %reshape.69), channel_id=1, source_target_pairs={{0,16},{1,48},{2,80},{3,112},{4,144},{5,176},{6,208},{7,240},{8,24... | collective-permute-start | bytes 294920 | tf_op jit(solution)/shard_map/ppermute | solution.py:94
  21.6 49.3 %collective-permute-start.9 = (bf16[48,1024]{1,0:T(8,128)(2,1)}, bf16[48,1024]{1,0:T(8,128)(2,1)S(1)}, u32[]{:S(2)}, u32[]{:S(2)}) collective-permute-start(bf16[48,1024]{1,0:T(8,128)(2,1)} %reshape.68), channel_id=1, source_target_pairs={{0,24},{1,56},{2,88},{3,120},{4,152},{5,184},{6,216},{7,248},{8,0}... | collective-permute-start | bytes 294920 | tf_op jit(solution)/shard_map/ppermute | solution.py:94
  29.3 9.3 %copy-start.13 = (bf16[3,3,48,48]{3,2,1,0:T(8,128)(2,1)S(1)}, bf16[3,3,48,48]{3,2,1,0:T(8,128)(2,1)}, u32[]{:S(2)}) copy-start(bf16[3,3,48,48]{3,2,1,0:T(8,128)(2,1)} %param.7) | copy-start | bytes 124420
  30.4 18.7 %collective-permute-start.3 = (bf16[48,48,8]{1,2,0:T(8,128)(2,1)S(1)}, bf16[48,48,8]{1,2,0:T(8,128)(2,1)}, u32[]{:S(2)}, u32[]{:S(2)}) collective-permute-start(bf16[48,48,8]{1,2,0:T(8,128)(2,1)S(1)} %copy.125), channel_id=1, source_target_pairs={{1,0},{2,1},{3,2},{4,3},{5,4},{6,5},{7,6},{9,8},{10,9},{11,10},{12... | collective-permute-start | bytes 110600 | tf_op jit(solution)/shard_map/ppermute | solution.py:21
  32.3 8.5 %collective-permute-start.2 = (bf16[48,48,8]{1,2,0:T(8,128)(2,1)S(1)}, bf16[48,48,8]{1,2,0:T(8,128)(2,1)S(1)}, u32[]{:S(2)}, u32[]{:S(2)}) collective-permute-start(bf16[48,48,8]{1,2,0:T(8,128)(2,1)S(1)} %copy.121), channel_id=1, source_target_pairs={{0,1},{1,2},{2,3},{3,4},{4,5},{5,6},{6,7},{8,9},{9,10},{10,11},{11... | collective-permute-start | bytes 110600 | tf_op jit(solution)/shard_map/ppermute | solution.py:20
  40.8 36.7 %collective-permute-start.8 = (bf16[48,1024]{1,0:T(8,128)(2,1)S(1)}, bf16[48,1024]{1,0:T(8,128)(2,1)S(1)}, u32[]{:S(2)}, u32[]{:S(2)}) collective-permute-start(bf16[48,1024]{1,0:T(8,128)(2,1)S(1)} %reshape.67), channel_id=1, source_target_pairs={{0,0},{1,32},{2,64},{3,96},{4,128},{5,160},{6,192},{7,224},{8,8},{... | collective-permute-start | bytes 294920 | tf_op jit(solution)/shard_map/ppermute | solution.py:94
  51.3 2.3 %copy-start.6 = (bf16[48,48,136]{2,0,1:T(8,128)(2,1)}, bf16[48,48,136]{2,0,1:T(8,128)(2,1)S(1)}, u32[]{:S(2)}) copy-start(bf16[48,48,136]{2,0,1:T(8,128)(2,1)S(1)} %get-tuple-element.34) | copy-start | bytes 1880068
  51.3 2.6 %copy-start.8 = (bf16[48,48,136]{2,0,1:T(8,128)(2,1)}, bf16[48,48,136]{2,0,1:T(8,128)(2,1)S(1)}, u32[]{:S(2)}) copy-start(bf16[48,48,136]{2,0,1:T(8,128)(2,1)S(1)} %get-tuple-element.33) | copy-start | bytes 1880068
  52.3 1.0 copy-start.4
  56.6 1.0 copy-start.10
  58.9 18.9 %collective-permute-start.7 = (bf16[48,1024]{1,0:T(8,128)(2,1)S(1)}, bf16[48,1024]{1,0:T(8,128)(2,1)S(1)}, u32[]{:S(2)}, u32[]{:S(2)}) collective-permute-start(bf16[48,1024]{1,0:T(8,128)(2,1)S(1)} %reshape.65), channel_id=1, source_target_pairs={{0,8},{1,40},{2,72},{3,104},{4,136},{5,168},{6,200},{7,232},{8,16}... | collective-permute-start | bytes 294920 | tf_op jit(solution)/shard_map/ppermute | solution.py:94
  62.3 15.6 %collective-permute-start.6 = (bf16[48,1024]{1,0:T(8,128)(2,1)S(1)}, bf16[48,1024]{1,0:T(8,128)(2,1)S(1)}, u32[]{:S(2)}, u32[]{:S(2)}) collective-permute-start(bf16[48,1024]{1,0:T(8,128)(2,1)S(1)} %reshape.64), channel_id=1, source_target_pairs={{0,16},{1,48},{2,80},{3,112},{4,144},{5,176},{6,208},{7,240},{8,24... | collective-permute-start | bytes 294920 | tf_op jit(solution)/shard_map/ppermute | solution.py:94
  67.7 29.4 %collective-permute-start.5 = (bf16[48,1024]{1,0:T(8,128)(2,1)S(1)}, bf16[48,1024]{1,0:T(8,128)(2,1)S(1)}, u32[]{:S(2)}, u32[]{:S(2)}) collective-permute-start(bf16[48,1024]{1,0:T(8,128)(2,1)S(1)} %reshape.63), channel_id=1, source_target_pairs={{0,24},{1,56},{2,88},{3,120},{4,152},{5,184},{6,216},{7,248},{8,0}... | collective-permute-start | bytes 294920 | tf_op jit(solution)/shard_map/ppermute | solution.py:94
  70.9 28.4 %collective-permute-start.4 = (bf16[48,1024]{1,0:T(8,128)(2,1)S(1)}, bf16[48,1024]{1,0:T(8,128)(2,1)S(1)}, u32[]{:S(2)}, u32[]{:S(2)}) collective-permute-start(bf16[48,1024]{1,0:T(8,128)(2,1)S(1)} %reshape.62), channel_id=1, source_target_pairs={{0,0},{1,32},{2,64},{3,96},{4,128},{5,160},{6,192},{7,224},{8,8},{... | collective-permute-start | bytes 294920 | tf_op jit(solution)/shard_map/ppermute | solution.py:94
  104.9 1.6 copy-start.2
  107.9 10.2 %copy-start.7 = (bf16[48,48,136]{2,0,1:T(8,128)(2,1)S(1)}, bf16[48,48,136]{2,0,1:T(8,128)(2,1)}, u32[]{:S(2)}) copy-start(bf16[48,48,136]{2,0,1:T(8,128)(2,1)} %copy-done.6) | copy-start | bytes 1880068
  109.9 8.5 %copy-start.9 = (bf16[48,48,136]{2,0,1:T(8,128)(2,1)S(1)}, bf16[48,48,136]{2,0,1:T(8,128)(2,1)}, u32[]{:S(2)}) copy-start(bf16[48,48,136]{2,0,1:T(8,128)(2,1)} %copy-done.8) | copy-start | bytes 1880068
  109.9 64.8 %collective-permute-start.12 = (bf16[48,8,128]{2,0,1:T(8,128)(2,1)}, bf16[48,8,128]{2,0,1:T(8,128)(2,1)}, u32[]{:S(2)}, u32[]{:S(2)}) collective-permute-start(bf16[48,8,128]{2,0,1:T(8,128)(2,1)} %get-tuple-element.37), channel_id=1, source_target_pairs={{0,8},{8,16},{16,24},{24,32},{32,40},{40,48},{48,56},{56,64},{64,7... | collective-permute-start | bytes 294920 | tf_op jit(solution)/shard_map/ppermute | solution.py:20
  113.1 5.5 %copy-start.5 = (bf16[48,32,128]{2,1,0:T(8,128)(2,1)S(1)}, bf16[48,32,128]{2,1,0:T(8,128)(2,1)}, u32[]{:S(2)}) copy-start(bf16[48,32,128]{2,1,0:T(8,128)(2,1)} %param.6) | copy-start | bytes 1179652
  113.1 61.5 %collective-permute-start.13 = (bf16[48,8,128]{2,0,1:T(8,128)(2,1)}, bf16[48,8,128]{2,0,1:T(8,128)(2,1)}, u32[]{:S(2)}, u32[]{:S(2)}) collective-permute-start(bf16[48,8,128]{2,0,1:T(8,128)(2,1)} %get-tuple-element.38), channel_id=1, source_target_pairs={{8,0},{16,8},{24,16},{32,24},{40,32},{48,40},{56,48},{64,56},{72,6... | collective-permute-start | bytes 294920 | tf_op jit(solution)/shard_map/ppermute | solution.py:21
  168.7 1.5 copy-start.11
  175.9 8.7 %copy-start.14 = (bf16[3,3,48,48]{3,2,1,0:T(8,128)(2,1)S(1)}, bf16[3,3,48,48]{3,2,1,0:T(8,128)(2,1)}, u32[]{:S(2)}) copy-start(bf16[3,3,48,48]{3,2,1,0:T(8,128)(2,1)} %param.7) | copy-start | bytes 124420
  177.0 12.1 %collective-permute-start.15 = (bf16[48,48,8]{1,2,0:T(8,128)(2,1)S(1)}, bf16[48,48,8]{1,2,0:T(8,128)(2,1)S(1)}, u32[]{:S(2)}, u32[]{:S(2)}) collective-permute-start(bf16[48,48,8]{1,2,0:T(8,128)(2,1)S(1)} %copy.161), channel_id=1, source_target_pairs={{0,1},{1,2},{2,3},{3,4},{4,5},{5,6},{6,7},{8,9},{9,10},{10,11},{11... | collective-permute-start | bytes 110600 | tf_op jit(solution)/shard_map/ppermute | solution.py:20
  178.9 8.9 %collective-permute-start.14 = (bf16[48,48,8]{1,2,0:T(8,128)(2,1)S(1)}, bf16[48,48,8]{1,2,0:T(8,128)(2,1)S(1)}, u32[]{:S(2)}, u32[]{:S(2)}) collective-permute-start(bf16[48,48,8]{1,2,0:T(8,128)(2,1)S(1)} %copy.157), channel_id=1, source_target_pairs={{1,0},{2,1},{3,2},{4,3},{5,4},{6,5},{7,6},{9,8},{10,9},{11,10},{12... | collective-permute-start | bytes 110600 | tf_op jit(solution)/shard_map/ppermute | solution.py:21
  192.5 1.1 copy-start.12
  194.8 1.0 copy-start.3
where the time goes:
time: 199 us; the launch traced here: 197 us
  starting transfers between devices  66.9 us (34%)
  Pallas kernels  45.5 us (23%)
  local copies, waits for them, and re-layouts  27.7 us (14%)
  waiting for transfers between devices  23 us (12%)
  matrix products  16.4 us (8%)
  other arithmetic  16.2 us (8%)
    pallas_call x1, Pallas kernels, all_sum(): pl.pallas_call(functools.partial(sum_kernel, strides), out_shape=jax.Shap...  45.5 us
    ppermute x8, starting transfers between devices, mirror_tile(): lax.ppermute(piece, ('row', 'col'), pairs).reshape(chans, rows, rows)  33.8 us
    ppermute x8, waiting for transfers between devices, mirror_tile(): lax.ppermute(piece, ('row', 'col'), pairs).reshape(chans, rows, rows)  21.1 us
    ppermute x4, starting transfers between devices, with_halo(): after = lax.ppermute(initial, axis, down)  19.8 us
    ppermute x4, starting transfers between devices, with_halo(): before = lax.ppermute(last, axis, up)  13.4 us
    transpose x10, local copies, waits for them, and re-layouts, mirror_tile(): piece = jnp.swapaxes(pieces[:, :, k, :], 1, 2).reshape(chans, rows * rows)  5.89 us
    dot_general x9, matrix products, shards(): jnp.einsum('io,ohw->ihw', kernel[row_tap, col_tap], piece, preferred_elem...  5.32 us
    unnamed x33, local copies, waits for them, and re-layouts  4.72 us
  transfers between devices with their start and end apart: 16, of which 4 were waited for; matrix products, arithmetic and copies ran while one was open for 19% of the time, Pallas kernels for 23%

commit v1 on v0

--- a/solution.py
+++ b/solution.py
@@ -75,25 +75,87 @@
     )(x)
 
 
+def mirror_kernel(group, slabs_ref, out_ref, send_sem, recv_sem, local_sem):
+    row, col = lax.axis_index("row"), lax.axis_index("col")
+    turn = row % group
+    own = row // group == col
+    targets = [(group * col + (turn + k) % group, row // group) for k in range(group)]
+    sources = [(group * col + (turn - k + group) % group, row // group) for k in range(group)]
+    barrier = pltpu.get_barrier_semaphore()
+    for k in range(group):
+        if k == 0:
+            @pl.when(jnp.logical_not(own))
+            def _():
+                pl.semaphore_signal(barrier, inc=1, device_id=sources[0], device_id_type=pl.DeviceIdType.MESH)
+        else:
+            pl.semaphore_signal(barrier, inc=1, device_id=sources[k], device_id_type=pl.DeviceIdType.MESH)
+    pl.semaphore_wait(barrier, group - own.astype(jnp.int32))
+    copies = []
+    for k in range(group):
+        copy = pltpu.make_async_remote_copy(
+            src_ref=slabs_ref.at[k],
+            dst_ref=out_ref.at[turn],
+            send_sem=send_sem.at[k],
+            recv_sem=recv_sem.at[k],
+            device_id=targets[k],
+            device_id_type=pl.DeviceIdType.MESH,
+        )
+        landing = pltpu.make_async_remote_copy(
+            src_ref=slabs_ref.at[k],
+            dst_ref=out_ref.at[(turn - k + group) % group],
+            send_sem=send_sem.at[k],
+            recv_sem=recv_sem.at[k],
+            device_id=sources[k],
+            device_id_type=pl.DeviceIdType.MESH,
+        )
+        copies.append((copy, landing))
+    local = pltpu.make_async_copy(slabs_ref.at[0], out_ref.at[turn], local_sem)
+
+    @pl.when(own)
+    def _():
+        local.start()
+
+    @pl.when(jnp.logical_not(own))
+    def _():
+        copies[0][0].start()
+
+    for copy, _ in copies[1:]:
+        copy.start()
+
+    @pl.when(own)
+    def _():
+        local.wait()
+
+    @pl.when(jnp.logical_not(own))
+    def _():
+        copies[0][0].wait_send()
+        copies[0][1].wait_recv()
+
+    for copy, landing in copies[1:]:
+        copy.wait_send()
+        landing.wait_recv()
+
+
 def mirror_tile(tile):
-    row_count = lax.axis_size("row")
-    col_count = lax.axis_size("col")
     chans, rows, cols = tile.shape
     group = cols // rows
     turn = lax.axis_index("row") % group
     pieces = jnp.roll(tile.reshape(chans, rows, group, rows), -turn, axis=2)
-    landed = []
-    for k in range(group):
-        piece = jnp.swapaxes(pieces[:, :, k, :], 1, 2).reshape(chans, rows * rows)
-        pairs = []
-        for source_row in range(row_count):
-            for source_col in range(col_count):
-                target_row = group * source_col + (source_row % group + k) % group
-                target = target_row * col_count + source_row // group
-                pairs.append((source_row * col_count + source_col, target))
-        landed.append(lax.ppermute(piece, ("row", "col"), pairs).reshape(chans, rows, rows))
-    slots = jnp.stack([landed[(-i) % group] for i in range(group)], axis=2)
-    return jnp.roll(slots, turn, axis=2).reshape(chans, rows, cols)
+    slabs = jnp.stack([jnp.swapaxes(pieces[:, :, k, :], 1, 2).reshape(chans, rows * rows) for k in range(group)])
+    landed = pl.pallas_call(
+        functools.partial(mirror_kernel, group),
+        out_shape=jax.ShapeDtypeStruct(slabs.shape, slabs.dtype),
+        in_specs=[pl.BlockSpec(memory_space=pltpu.VMEM)],
+        out_specs=pl.BlockSpec(memory_space=pltpu.VMEM),
+        scratch_shapes=[
+            pltpu.SemaphoreType.DMA((group,)),
+            pltpu.SemaphoreType.DMA((group,)),
+            pltpu.SemaphoreType.DMA,
+        ],
+        compiler_params=pltpu.CompilerParams(collective_id=1, has_side_effects=True),
+    )(slabs)
+    landed = landed.reshape(group, chans, rows, rows)
+    return jnp.transpose(landed, (1, 2, 0, 3)).reshape(chans, rows, cols)
 
 
 def window(padded, top, left, rows, cols):

time: 199 us -> 249 us (1.25)
  Pallas kernels: 45.5 us -> 130 us
  starting transfers between devices: 66.9 us -> 33 us
  waiting for transfers between devices: 23 us -> 3.6 us
  local copies, waits for them, and re-layouts: 27.7 us -> 42.5 us
  matrix products: 16.4 us -> 22.4 us
    pallas_call x0 -> x2, Pallas kernels: none -> 88.2 us  [mirror_tile(): pl.pallas_call(functools.partial(mirror_kernel, group), out_shape=jax.Sha...]
    ppermute x8 -> x0, starting transfers between devices: 33.8 us -> none  [mirror_tile(): lax.ppermute(piece, ('row', 'col'), pairs).reshape(chans, rows, rows)]
    ppermute x8 -> x0, waiting for transfers between devices: 21.1 us -> none  [mirror_tile(): lax.ppermute(piece, ('row', 'col'), pairs).reshape(chans, rows, rows)]
    dot_general x9, matrix products: 3.37 us -> 9.83 us  [shards(): jnp.einsum('ihw,ohw->io', piece, grad_before, preferred_element_type=jnp....]
    convert_element_type x1 -> x3, local copies, waits for them, and re-layouts: 0.58 us -> 6.93 us  [shards(): grad_turned.astype(jnp.float32)]
    convert_element_type x1 -> x3, local copies, waits for them, and re-layouts: 1.47 us -> 6.95 us  [shards(): mixed_turned.astype(jnp.float32)]
    concatenate x1 -> x0, other arithmetic: 4.53 us -> none  [mirror_tile(): return jnp.roll(slots, turn, axis=2).reshape(chans, rows, cols)]
    reshape x8 -> x0, local copies, waits for them, and re-layouts: 3.83 us -> none  [mirror_tile(): piece = jnp.swapaxes(pieces[:, :, k, :], 1, 2).reshape(chans, rows * rows)]
  transfers between devices with their start and end apart: 16 -> 8, of which waited for: 4 -> 3; matrix products, arithmetic and copies ran while one was open for 19% -> 9% of each run, Pallas kernels for 23% -> 17%
where the time goes in v1:
time: 249 us; the launch traced here: 248 us
  Pallas kernels  130 us (52%)
  local copies, waits for them, and re-layouts  42.5 us (17%)
  starting transfers between devices  33 us (13%)
  matrix products  22.4 us (9%)
  other arithmetic  14.5 us (6%)
  waiting for transfers between devices  3.6 us (1%)
    pallas_call x2, Pallas kernels, mirror_tile(): pl.pallas_call(functools.partial(mirror_kernel, group), out_shape=jax.Sha...  88.2 us
    pallas_call x1, Pallas kernels, all_sum(): pl.pallas_call(functools.partial(sum_kernel, strides), out_shape=jax.Shap...  42.1 us
    ppermute x4, starting transfers between devices, with_halo(): after = lax.ppermute(initial, axis, down)  21.2 us
    ppermute x4, starting transfers between devices, with_halo(): before = lax.ppermute(last, axis, up)  11.8 us
    dot_general x9, matrix products, shards(): jnp.einsum('ihw,ohw->io', piece, grad_before, preferred_element_type=jnp....  9.83 us
    convert_element_type x3, local copies, waits for them, and re-layouts, shards(): mixed_turned.astype(jnp.float32)  6.95 us
    convert_element_type x3, local copies, waits for them, and re-layouts, shards(): grad_turned.astype(jnp.float32)  6.93 us
    dot_general x9, matrix products, shards(): jnp.einsum('io,ihw->ohw', kernel[row_tap, col_tap], piece, preferred_elem...  6.6 us
  transfers between devices with their start and end apart: 8, of which 3 were waited for; matrix products, arithmetic and copies ran while one was open for 9% of the time, Pallas kernels for 17%

profile of v1, /device:TPU:6, one launch (start us, length us, event | category | flops | bytes accessed | tf_op | source)
XLA Modules:
  0.0 247.7 jit_solution(3720344868961310333)
XLA Ops:
  0.7 1.2 copy_maximum_fusion
  1.9 1.9 collective-permute-start
  3.8 7.5 %collective-permute-start.1 = (bf16[48,8,128]{2,0,1:T(8,128)(2,1)S(1)}, bf16[48,8,128]{2,0,1:T(8,128)(2,1)S(1)}, u32[]{:S(2)}, u32[]{:S(2)}) collective-permute-start(bf16[48,8,128]{2,0,1:T(8,128)(2,1)S(1)} %get-tuple-element.36), channel_id=1, source_target_pairs={{8,0},{16,8},{24,16},{32,24},{40,32},{48,40},{56,48},{64,56},{72,6... | collective-permute-start | bytes 294920 | tf_op jit(solution)/shard_map/ppermute | solution.py:21
  11.3 1.5 copy.103
  15.5 3.1 %collective-permute-start.3 = (bf16[48,48,8]{1,2,0:T(8,128)(2,1)S(1)}, bf16[48,48,8]{1,2,0:T(8,128)(2,1)S(1)}, u32[]{:S(2)}, u32[]{:S(2)}) collective-permute-start(bf16[48,48,8]{1,2,0:T(8,128)(2,1)S(1)} %copy.84), channel_id=1, source_target_pairs={{1,0},{2,1},{3,2},{4,3},{5,4},{6,5},{7,6},{9,8},{10,9},{11,10},{12... | collective-permute-start | bytes 110600 | tf_op jit(solution)/shard_map/ppermute | solution.py:21
  18.6 5.2 %collective-permute-start.2 = (bf16[48,48,8]{1,2,0:T(8,128)(2,1)S(1)}, bf16[48,48,8]{1,2,0:T(8,128)(2,1)S(1)}, u32[]{:S(2)}, u32[]{:S(2)}) collective-permute-start(bf16[48,48,8]{1,2,0:T(8,128)(2,1)S(1)} %copy.80), channel_id=1, source_target_pairs={{0,1},{1,2},{2,3},{3,4},{4,5},{5,6},{6,7},{8,9},{9,10},{10,11},{11... | collective-permute-start | bytes 110600 | tf_op jit(solution)/shard_map/ppermute | solution.py:20
  23.8 1.9 fusion.50
  25.7 0.9 collective-permute-done.2
  26.6 1.3 copy.81
  27.9 1.3 copy.85
  29.2 2.1 maximum_maximum_fusion
  31.3 1.1 fusion.55
  33.1 1.0 convolution_add_fusion.12
  34.1 1.1 convolution_add_fusion.11
  38.5 1.3 copy.94
  39.8 3.3 %fusion.22 = (bf16[48,32,4,32]{0,3,2,1:T(8,128)(2,1)S(1)}, bf16[48,32,4,32]{0,3,2,1:T(8,128)(2,1)}) fusion(s32[]{:T(128)S(6)} %select_n.31, bf16[48,32,4,32]{0,3,2,1:T(8,128)(2,1)S(1)} %bitcast.217, bf16[48,32,4,32]{0,3,2,1:T(8,128)(2,1)} %bitcast.218), kind=kLoop, calls=%fused_computation.55 | loop fusion | flops 393216 | bytes 1572868 | tf_op jit(solution)/shard_map/jit(_roll_dynamic)/concatenate | solution.py:143
  43.2 0.7 copy.104
  44.3 0.7 copy.106
  45.4 0.7 copy.105
  46.6 0.7 copy.107
  47.7 0.8 pad_maximum_fusion.5.slabs_ref
  48.5 47.6 %shard_map.76 = bf16[4,48,1024]{2,1,0:T(8,128)(2,1)} custom-call(bf16[4,48,1024]{2,1,0:T(8,128)(2,1)} %pad_maximum_fusion.5.slabs_ref), custom_call_target="tpu_custom_call" | custom-call | tf_op jit(solution)/shard_map/pallas_call | solution.py:145
  96.1 2.1 reshape.50
  98.2 2.6 %copy.108 = f32[48,32,4,32]{0,3,2,1:T(8,128)} copy(f32[48,32,4,32]{3,1,0,2:T(8,128)S(1)} %bitcast.213) | data formatting | bytes 1572864 | tf_op jit(solution)/shard_map/convert_element_type | solution.py:188
  100.8 2.2 copy.109
  103.0 0.9 convolution_bitcast_fusion.3
  105.0 1.8 fusion.21
  106.9 0.7 copy.95
  108.1 0.7 copy.97
  109.2 0.7 copy.96
  110.3 0.7 copy.98
  111.4 0.8 pad_maximum_fusion.4.slabs_ref
  112.2 40.6 %shard_map.75 = bf16[4,48,1024]{2,1,0:T(8,128)(2,1)} custom-call(bf16[4,48,1024]{2,1,0:T(8,128)(2,1)} %pad_maximum_fusion.4.slabs_ref), custom_call_target="tpu_custom_call" | custom-call | tf_op jit(solution)/shard_map/pallas_call | solution.py:145
  152.9 2.1 reshape.49
  154.9 2.6 %copy.99 = f32[48,32,4,32]{0,3,2,1:T(8,128)} copy(f32[48,32,4,32]{3,1,0,2:T(8,128)S(1)} %bitcast.214) | data formatting | bytes 1572864 | tf_op jit(solution)/shard_map/convert_element_type | solution.py:185
  157.6 2.2 copy.100
  159.9 0.9 add_convert_fusion
  160.8 1.5 reshape.45
  162.3 1.9 collective-permute-start.4
  164.3 6.0 %collective-permute-start.5 = (bf16[48,8,128]{2,0,1:T(8,128)(2,1)}, bf16[48,8,128]{2,0,1:T(8,128)(2,1)}, u32[]{:S(2)}, u32[]{:S(2)}) collective-permute-start(bf16[48,8,128]{2,0,1:T(8,128)(2,1)} %get-tuple-element.34), channel_id=1, source_target_pairs={{8,0},{16,8},{24,16},{32,24},{40,32},{48,40},{56,48},{64,56},{72,6... | collective-permute-start | bytes 294920 | tf_op jit(solution)/shard_map/ppermute | solution.py:21
  170.2 1.7 fusion.14
  172.0 0.9 fusion.20
  172.9 0.9 fusion.19
  173.8 0.9 fusion.18
  174.7 0.9 fusion.17
  175.6 0.8 fusion.16
  176.5 0.9 fusion.13
  177.3 0.9 fusion.15
  178.2 1.1 reshape_reshape.3
  180.0 42.1 %shard_map.77 = f32[180,128]{1,0:T(8,128)} custom-call(f32[180,128]{1,0:T(8,128)} %maximum_bitcast_fusion.x_ref), custom_call_target="tpu_custom_call" | custom-call | tf_op jit(solution)/shard_map/pallas_call | solution.py:63
  222.1 0.9 slice_multiply_fusion
  223.0 0.7 slice_multiply_fusion.1
  223.7 0.8 copy.123
  225.3 0.8 div.18
  226.1 1.0 pad_maximum_fusion.3
  228.4 2.8 %collective-permute-start.7 = (bf16[48,48,8]{1,2,0:T(8,128)(2,1)S(1)}, bf16[48,48,8]{1,2,0:T(8,128)(2,1)S(1)}, u32[]{:S(2)}, u32[]{:S(2)}) collective-permute-start(bf16[48,48,8]{1,2,0:T(8,128)(2,1)S(1)} %copy.114), channel_id=1, source_target_pairs={{0,1},{1,2},{2,3},{3,4},{4,5},{5,6},{6,7},{8,9},{9,10},{10,11},{11... | collective-permute-start | bytes 110600 | tf_op jit(solution)/shard_map/ppermute | solution.py:20
  231.2 4.6 %collective-permute-start.6 = (bf16[48,48,8]{1,2,0:T(8,128)(2,1)S(1)}, bf16[48,48,8]{1,2,0:T(8,128)(2,1)S(1)}, u32[]{:S(2)}, u32[]{:S(2)}) collective-permute-start(bf16[48,48,8]{1,2,0:T(8,128)(2,1)S(1)} %copy.110), channel_id=1, source_target_pairs={{1,0},{2,1},{3,2},{4,3},{5,4},{6,5},{7,6},{9,8},{10,9},{11,10},{12... | collective-permute-start | bytes 110600 | tf_op jit(solution)/shard_map/ppermute | solution.py:21
  235.8 1.1 fusion.32
  236.9 1.1 fusion.36
  238.0 2.0 collective-permute-done.6
  240.6 1.3 copy.115
  241.8 2.0 pad_maximum_fusion.1
  245.5 0.7 copy-done.4
  246.9 0.8 copy.124
  (95 shorter events, 16.1 us)
Async XLA Ops:
  0.6 37.5 %copy-start = (bf16[48,48]{1,0:T(8,128)(2,1)S(1)}, bf16[48,48]{1,0:T(8,128)(2,1)}, u32[]{:S(2)}) copy-start(bf16[48,48]{1,0:T(8,128)(2,1)} %param.8) | copy-start | bytes 13828
  0.6 10.7 %copy-start.3 = (bf16[48,32,128]{2,1,0:T(8,128)(2,1)S(1)}, bf16[48,32,128]{2,1,0:T(8,128)(2,1)}, u32[]{:S(2)}) copy-start(bf16[48,32,128]{2,1,0:T(8,128)(2,1)} %param.9) | copy-start | bytes 1179652
  1.8 35.4 %copy-start.1 = (bf16[48,32,128]{2,0,1:T(8,128)(2,1)}, bf16[48,32,128]{2,0,1:T(8,128)(2,1)S(1)}, u32[]{:S(2)}) copy-start(bf16[48,32,128]{2,0,1:T(8,128)(2,1)S(1)} %copy_maximum_fusion) | copy-start | bytes 1179652
  1.9 11.0 %collective-permute-start = (bf16[48,8,128]{2,0,1:T(8,128)(2,1)S(1)}, bf16[48,8,128]{2,0,1:T(8,128)(2,1)S(1)}, u32[]{:S(2)}, u32[]{:S(2)}) collective-permute-start(bf16[48,8,128]{2,0,1:T(8,128)(2,1)S(1)} %get-tuple-element.35), channel_id=1, source_target_pairs={{0,8},{8,16},{16,24},{24,32},{32,40},{40,48},{48,56},{56,64},{64,7... | collective-permute-start | bytes 294920 | tf_op jit(solution)/shard_map/ppermute | solution.py:20
  3.8 9.7 %collective-permute-start.1 = (bf16[48,8,128]{2,0,1:T(8,128)(2,1)S(1)}, bf16[48,8,128]{2,0,1:T(8,128)(2,1)S(1)}, u32[]{:S(2)}, u32[]{:S(2)}) collective-permute-start(bf16[48,8,128]{2,0,1:T(8,128)(2,1)S(1)} %get-tuple-element.36), channel_id=1, source_target_pairs={{8,0},{16,8},{24,16},{32,24},{40,32},{48,40},{56,48},{64,56},{72,6... | collective-permute-start | bytes 294920 | tf_op jit(solution)/shard_map/ppermute | solution.py:21
  12.8 15.1 %copy-start.23 = (bf16[48,8,128]{2,0,1:T(8,128)(2,1)}, bf16[48,8,128]{2,0,1:T(8,128)(2,1)S(1)}, u32[]{:S(2)}) copy-start(bf16[48,8,128]{2,0,1:T(8,128)(2,1)S(1)} %collective-permute-done) | copy-start | bytes 294916
  13.5 0.6 copy-start.19
  15.5 13.7 %copy-start.20 = (bf16[48,8,128]{2,0,1:T(8,128)(2,1)S(1)}, bf16[48,8,128]{2,0,1:T(8,128)(2,1)}, u32[]{:S(2)}) copy-start(bf16[48,8,128]{2,0,1:T(8,128)(2,1)} %copy-done.19) | copy-start | bytes 294916
  15.5 12.5 %collective-permute-start.3 = (bf16[48,48,8]{1,2,0:T(8,128)(2,1)S(1)}, bf16[48,48,8]{1,2,0:T(8,128)(2,1)S(1)}, u32[]{:S(2)}, u32[]{:S(2)}) collective-permute-start(bf16[48,48,8]{1,2,0:T(8,128)(2,1)S(1)} %copy.84), channel_id=1, source_target_pairs={{1,0},{2,1},{3,2},{4,3},{5,4},{6,5},{7,6},{9,8},{10,9},{11,10},{12... | collective-permute-start | bytes 110600 | tf_op jit(solution)/shard_map/ppermute | solution.py:21
  18.6 8.0 %collective-permute-start.2 = (bf16[48,48,8]{1,2,0:T(8,128)(2,1)S(1)}, bf16[48,48,8]{1,2,0:T(8,128)(2,1)S(1)}, u32[]{:S(2)}, u32[]{:S(2)}) collective-permute-start(bf16[48,48,8]{1,2,0:T(8,128)(2,1)S(1)} %copy.80), channel_id=1, source_target_pairs={{0,1},{1,2},{2,3},{3,4},{4,5},{5,6},{6,7},{8,9},{9,10},{10,11},{11... | collective-permute-start | bytes 110600 | tf_op jit(solution)/shard_map/ppermute | solution.py:20
  31.3 5.2 %copy-start.9 = (bf16[48,48,136]{2,0,1:T(8,128)(2,1)}, bf16[48,48,136]{2,0,1:T(8,128)(2,1)S(1)}, u32[]{:S(2)}) copy-start(bf16[48,48,136]{2,0,1:T(8,128)(2,1)S(1)} %get-tuple-element.30) | copy-start | bytes 1880068
  31.3 5.6 %copy-start.11 = (bf16[48,48,136]{2,0,1:T(8,128)(2,1)}, bf16[48,48,136]{2,0,1:T(8,128)(2,1)S(1)}, u32[]{:S(2)}) copy-start(bf16[48,48,136]{2,0,1:T(8,128)(2,1)S(1)} %get-tuple-element.29) | copy-start | bytes 1880068
  31.3 1.8 copy-start.17
  34.1 1.1 copy-start.24
  35.2 1.0 copy-start.5
  36.9 0.9 copy-start.21
  38.1 5.0 %copy-start.7 = (bf16[48,32,128]{2,0,1:T(8,128)(2,1)}, bf16[48,32,128]{2,0,1:T(8,128)(2,1)S(1)}, u32[]{:S(2)}) copy-start(bf16[48,32,128]{2,0,1:T(8,128)(2,1)S(1)} %fusion.11) | copy-start | bytes 1179652
  38.1 1.7 copy-start.13
  38.4 4.6 %copy-start.15 = (bf16[48,32,128]{2,0,1:T(8,128)(2,1)}, bf16[48,32,128]{2,0,1:T(8,128)(2,1)S(1)}, u32[]{:S(2)}) copy-start(bf16[48,32,128]{2,0,1:T(8,128)(2,1)S(1)} %fusion.12) | copy-start | bytes 1179652
  100.8 2.2 copy-start.8
  104.0 2.9 %copy-start.14 = (bf16[48,32,4,32]{0,3,2,1:T(8,128)(2,1)S(1)}, bf16[48,32,4,32]{0,3,2,1:T(8,128)(2,1)}, u32[]{:S(2)}) copy-start(bf16[48,32,4,32]{0,3,2,1:T(8,128)(2,1)} %get-tuple-element.38) | copy-start | bytes 1179652
  157.6 2.3 copy-start.6
  157.6 2.3 copy-start.16
  159.9 10.4 %copy-start.2 = (bf16[48,32,128]{2,0,1:T(8,128)(2,1)S(1)}, bf16[48,32,128]{2,0,1:T(8,128)(2,1)}, u32[]{:S(2)}) copy-start(bf16[48,32,128]{2,0,1:T(8,128)(2,1)} %copy-done.1) | copy-start | bytes 1179652
  159.9 12.1 %copy-start.10 = (bf16[48,48,136]{2,0,1:T(8,128)(2,1)S(1)}, bf16[48,48,136]{2,0,1:T(8,128)(2,1)}, u32[]{:S(2)}) copy-start(bf16[48,48,136]{2,0,1:T(8,128)(2,1)} %copy-done.9) | copy-start | bytes 1880068
  160.8 12.1 %copy-start.12 = (bf16[48,48,136]{2,0,1:T(8,128)(2,1)S(1)}, bf16[48,48,136]{2,0,1:T(8,128)(2,1)}, u32[]{:S(2)}) copy-start(bf16[48,48,136]{2,0,1:T(8,128)(2,1)} %copy-done.11) | copy-start | bytes 1880068
  162.3 63.8 %collective-permute-start.4 = (bf16[48,8,128]{2,0,1:T(8,128)(2,1)}, bf16[48,8,128]{2,0,1:T(8,128)(2,1)}, u32[]{:S(2)}, u32[]{:S(2)}) collective-permute-start(bf16[48,8,128]{2,0,1:T(8,128)(2,1)} %get-tuple-element.33), channel_id=1, source_target_pairs={{0,8},{8,16},{16,24},{24,32},{32,40},{40,48},{48,56},{56,64},{64,7... | collective-permute-start | bytes 294920 | tf_op jit(solution)/shard_map/ppermute | solution.py:20
  164.3 61.8 %collective-permute-start.5 = (bf16[48,8,128]{2,0,1:T(8,128)(2,1)}, bf16[48,8,128]{2,0,1:T(8,128)(2,1)}, u32[]{:S(2)}, u32[]{:S(2)}) collective-permute-start(bf16[48,8,128]{2,0,1:T(8,128)(2,1)} %get-tuple-element.34), channel_id=1, source_target_pairs={{8,0},{16,8},{24,16},{32,24},{40,32},{48,40},{56,48},{64,56},{72,6... | collective-permute-start | bytes 294920 | tf_op jit(solution)/shard_map/ppermute | solution.py:21
  173.8 2.7 %copy-start.22 = (bf16[48,8,128]{2,0,1:T(8,128)(2,1)S(1)}, bf16[48,8,128]{2,0,1:T(8,128)(2,1)}, u32[]{:S(2)}) copy-start(bf16[48,8,128]{2,0,1:T(8,128)(2,1)} %copy-done.19) | copy-start | bytes 294916
  176.4 2.9 %copy-start.26 = (f32[2304]{0:T(1024)S(1)}, f32[2304]{0:T(1024)}, u32[]{:S(2)}) copy-start(f32[2304]{0:T(1024)} %reshape.45) | copy-start | bytes 27652
  176.4 47.3 %copy-start.18 = (bf16[48,32,128]{2,0,1:T(8,128)(2,1)S(1)}, bf16[48,32,128]{2,0,1:T(8,128)(2,1)}, u32[]{:S(2)}) copy-start(bf16[48,32,128]{2,0,1:T(8,128)(2,1)} %add_convert_fusion) | copy-start | bytes 1179652
  227.3 8.4 %copy-start.25 = (bf16[3,3,48,48]{3,2,1,0:T(8,128)(2,1)S(1)}, bf16[3,3,48,48]{3,2,1,0:T(8,128)(2,1)}, u32[]{:S(2)}) copy-start(bf16[3,3,48,48]{3,2,1,0:T(8,128)(2,1)} %param.7) | copy-start | bytes 124420
  228.4 12.2 %collective-permute-start.7 = (bf16[48,48,8]{1,2,0:T(8,128)(2,1)S(1)}, bf16[48,48,8]{1,2,0:T(8,128)(2,1)S(1)}, u32[]{:S(2)}, u32[]{:S(2)}) collective-permute-start(bf16[48,48,8]{1,2,0:T(8,128)(2,1)S(1)} %copy.114), channel_id=1, source_target_pairs={{0,1},{1,2},{2,3},{3,4},{4,5},{5,6},{6,7},{8,9},{9,10},{10,11},{11... | collective-permute-start | bytes 110600 | tf_op jit(solution)/shard_map/ppermute | solution.py:20
  231.2 8.9 %collective-permute-start.6 = (bf16[48,48,8]{1,2,0:T(8,128)(2,1)S(1)}, bf16[48,48,8]{1,2,0:T(8,128)(2,1)S(1)}, u32[]{:S(2)}, u32[]{:S(2)}) collective-permute-start(bf16[48,48,8]{1,2,0:T(8,128)(2,1)S(1)} %copy.110), channel_id=1, source_target_pairs={{1,0},{2,1},{3,2},{4,3},{5,4},{6,5},{7,6},{9,8},{10,9},{11,10},{12... | collective-permute-start | bytes 110600 | tf_op jit(solution)/shard_map/ppermute | solution.py:21
  245.3 1.0 copy-start.4

commit v2 on v0

--- a/solution.py
+++ b/solution.py
@@ -116,12 +116,7 @@
     mixed = jnp.einsum("io,ihw->ohw", mixing, hidden, preferred_element_type=jnp.float32).astype(
         jnp.bfloat16
     )
-    mixed_turned = mirror_tile(mixed)
     grad_turned = mirror_tile(cotangent)
-    output = (
-        maps.astype(jnp.float32)
-        + 0.5 * (mixed.astype(jnp.float32) + mixed_turned.astype(jnp.float32))
-    ).astype(jnp.bfloat16)
     grad_wide = cotangent.astype(jnp.float32)
     grad_mixed = (0.5 * (grad_wide + grad_turned.astype(jnp.float32))).astype(jnp.bfloat16)
     local_mixing = jnp.einsum("ihw,ohw->io", hidden, grad_mixed, preferred_element_type=jnp.float32)
@@ -137,8 +132,14 @@
     local_kernel = jnp.stack(tap_grads).reshape(3, 3, chans, chans)
     flat = jnp.concatenate([local_kernel.reshape(-1), local_mixing.reshape(-1)])
     sums = all_sum(flat.reshape(-1, 128)).reshape(-1)
+    sums, mixed = lax.optimization_barrier((sums, mixed))
     grad_kernel = sums[: 9 * chans * chans].reshape(3, 3, chans, chans)
     grad_mixing = sums[9 * chans * chans :].reshape(chans, chans)
+    mixed_turned = mirror_tile(mixed)
+    output = (
+        maps.astype(jnp.float32)
+        + 0.5 * (mixed.astype(jnp.float32) + mixed_turned.astype(jnp.float32))
+    ).astype(jnp.bfloat16)
     grad_padded = with_halo(grad_before, (("row", 1), ("col", 2)), DILATION)
     grad_active = jnp.zeros((chans, rows, cols), jnp.float32)
     for row_tap in range(3):

time: 199 us -> 206 us (1.035)
  local copies, waits for them, and re-layouts: 27.7 us -> 44.1 us
  Pallas kernels: 45.5 us -> 38.5 us
  waiting for transfers between devices: 23 us -> 19.4 us
  matrix products: 16.4 us -> 18.8 us
    pallas_call x1, Pallas kernels: 45.5 us -> 38.5 us  [all_sum(): pl.pallas_call(functools.partial(sum_kernel, strides), out_shape=jax.Shap...]
    dot_general x9, matrix products: 3.37 us -> 7.98 us  [shards(): jnp.einsum('ihw,ohw->io', piece, grad_before, preferred_element_type=jnp....]
    reshape x8, local copies, waits for them, and re-layouts: 3.83 us -> 8.33 us  [mirror_tile(): piece = jnp.swapaxes(pieces[:, :, k, :], 1, 2).reshape(chans, rows * rows)]
    ppermute x2, local copies, waits for them, and re-layouts: 1.75 us -> 4.3 us  [with_halo(): before = lax.ppermute(last, axis, up)]
    ppermute x8, starting transfers between devices: 33.8 us -> 31.7 us  [mirror_tile(): lax.ppermute(piece, ('row', 'col'), pairs).reshape(chans, rows, rows)]
    unnamed x33 -> x25, local copies, waits for them, and re-layouts: 4.72 us -> 6.54 us
    concatenate x1 -> x2, other arithmetic: 4.53 us -> 3.78 us  [mirror_tile(): return jnp.roll(slots, turn, axis=2).reshape(chans, rows, cols)]
  transfers between devices with their start and end apart: 16 -> 16, of which waited for: 4 -> 4; matrix products, arithmetic and copies ran while one was open for 19% -> 27% of each run, Pallas kernels for 23% -> 19%
where the time goes in v2:
time: 206 us; the launch traced here: 203 us
  starting transfers between devices  65.5 us (32%)
  local copies, waits for them, and re-layouts  44.1 us (21%)
  Pallas kernels  38.5 us (19%)
  waiting for transfers between devices  19.4 us (9%)
  matrix products  18.8 us (9%)
  other arithmetic  15.6 us (8%)
    pallas_call x1, Pallas kernels, all_sum(): pl.pallas_call(functools.partial(sum_kernel, strides), out_shape=jax.Shap...  38.5 us
    ppermute x8, starting transfers between devices, mirror_tile(): lax.ppermute(piece, ('row', 'col'), pairs).reshape(chans, rows, rows)  31.7 us
    ppermute x4, starting transfers between devices, with_halo(): after = lax.ppermute(initial, axis, down)  21.2 us
    ppermute x8, waiting for transfers between devices, mirror_tile(): lax.ppermute(piece, ('row', 'col'), pairs).reshape(chans, rows, rows)  19.3 us
    ppermute x4, starting transfers between devices, with_halo(): before = lax.ppermute(last, axis, up)  12.6 us
    reshape x8, local copies, waits for them, and re-layouts, mirror_tile(): piece = jnp.swapaxes(pieces[:, :, k, :], 1, 2).reshape(chans, rows * rows)  8.33 us
    dot_general x9, matrix products, shards(): jnp.einsum('ihw,ohw->io', piece, grad_before, preferred_element_type=jnp....  7.98 us
    unnamed x25, local copies, waits for them, and re-layouts  6.54 us
  transfers between devices with their start and end apart: 16, of which 4 were waited for; matrix products, arithmetic and copies ran while one was open for 27% of the time, Pallas kernels for 19%

profile of v2, /device:TPU:6, one launch (start us, length us, event | category | flops | bytes accessed | tf_op | source)
XLA Modules:
  0.0 203.1 jit_solution(2494110887473356878)
XLA Ops:
  0.7 1.2 copy_maximum_fusion
  2.5 1.9 collective-permute-start
  4.4 7.5 %collective-permute-start.1 = (bf16[48,8,128]{2,0,1:T(8,128)(2,1)}, bf16[48,8,128]{2,0,1:T(8,128)(2,1)S(1)}, u32[]{:S(2)}, u32[]{:S(2)}) collective-permute-start(bf16[48,8,128]{2,0,1:T(8,128)(2,1)} %get-tuple-element.44), channel_id=1, source_target_pairs={{8,0},{16,8},{24,16},{32,24},{40,32},{48,40},{56,48},{64,56},{72,6... | collective-permute-start | bytes 294920 | tf_op jit(solution)/shard_map/ppermute | solution.py:21
  14.0 1.0 reshape.71
  15.0 1.9 collective-permute-start.7
  17.6 1.0 reshape.70
  18.6 3.0 %collective-permute-start.6 = (bf16[48,1024]{1,0:T(8,128)(2,1)}, bf16[48,1024]{1,0:T(8,128)(2,1)S(1)}, u32[]{:S(2)}, u32[]{:S(2)}) collective-permute-start(bf16[48,1024]{1,0:T(8,128)(2,1)} %reshape.70), channel_id=1, source_target_pairs={{0,16},{1,48},{2,80},{3,112},{4,144},{5,176},{6,208},{7,240},{8,24... | collective-permute-start | bytes 294920 | tf_op jit(solution)/shard_map/ppermute | solution.py:94
  22.3 1.0 reshape.69
  23.4 6.3 %collective-permute-start.5 = (bf16[48,1024]{1,0:T(8,128)(2,1)}, bf16[48,1024]{1,0:T(8,128)(2,1)}, u32[]{:S(2)}, u32[]{:S(2)}) collective-permute-start(bf16[48,1024]{1,0:T(8,128)(2,1)} %reshape.69), channel_id=1, source_target_pairs={{0,24},{1,56},{2,88},{3,120},{4,152},{5,184},{6,216},{7,248},{8,0}... | collective-permute-start | bytes 294920 | tf_op jit(solution)/shard_map/ppermute | solution.py:94
  30.3 1.0 reshape.68
  31.4 1.9 collective-permute-start.4
  33.6 1.1 copy.121
  34.8 1.1 copy.125
  35.9 1.9 collective-permute-start.3
  37.8 6.5 %collective-permute-start.2 = (bf16[48,48,8]{1,2,0:T(8,128)(2,1)}, bf16[48,48,8]{1,2,0:T(8,128)(2,1)}, u32[]{:S(2)}, u32[]{:S(2)}) collective-permute-start(bf16[48,48,8]{1,2,0:T(8,128)(2,1)} %copy.121), channel_id=1, source_target_pairs={{0,1},{1,2},{2,3},{3,4},{4,5},{5,6},{6,7},{8,9},{9,10},{10,11},{11... | collective-permute-start | bytes 110600 | tf_op jit(solution)/shard_map/ppermute | solution.py:20
  44.7 6.2 %collective-permute-done.5 = bf16[48,1024]{1,0:T(8,128)(2,1)} collective-permute-done((bf16[48,1024]{1,0:T(8,128)(2,1)}, bf16[48,1024]{1,0:T(8,128)(2,1)}, u32[]{:S(2)}, u32[]{:S(2)}) %collective-permute-start.5) | collective-permute-done | bytes 98336 | tf_op jit(solution)/shard_map/ppermute | solution.py:94
  51.0 1.1 copy.183
  52.0 3.4 %collective-permute-done.4 = bf16[48,1024]{1,0:T(8,128)(2,1)S(1)} collective-permute-done((bf16[48,1024]{1,0:T(8,128)(2,1)}, bf16[48,1024]{1,0:T(8,128)(2,1)S(1)}, u32[]{:S(2)}, u32[]{:S(2)}) %collective-permute-start.4) | collective-permute-done | bytes 98336 | tf_op jit(solution)/shard_map/ppermute | solution.py:94
  55.6 1.9 fusion.33
  58.4 1.2 fusion.64
  59.6 1.5 copy.144
  61.1 2.1 %copy.122 = bf16[48,48,8]{2,0,1:T(8,128)(2,1)} copy(bf16[48,48,8]{1,2,0:T(8,128)(2,1)} %collective-permute-done.2) | data formatting | bytes 73728 | tf_op jit(solution)/shard_map/ppermute | solution.py:20
  63.2 2.2 %copy.126 = bf16[48,48,8]{2,0,1:T(8,128)(2,1)} copy(bf16[48,48,8]{1,2,0:T(8,128)(2,1)} %collective-permute-done.3) | data formatting | bytes 73728 | tf_op jit(solution)/shard_map/ppermute | solution.py:21
  65.4 2.0 maximum_maximum_fusion
  67.8 1.2 copy-done.8
  73.5 1.1 fusion.12
  75.2 0.9 fusion.21
  76.2 2.0 %collective-permute-start.12 = (bf16[48,8,128]{2,0,1:T(8,128)(2,1)}, bf16[48,8,128]{2,0,1:T(8,128)(2,1)}, u32[]{:S(2)}, u32[]{:S(2)}) collective-permute-start(bf16[48,8,128]{2,0,1:T(8,128)(2,1)} %get-tuple-element.41), channel_id=1, source_target_pairs={{0,8},{8,16},{16,24},{24,32},{32,40},{40,48},{48,56},{56,64},{64,7... | collective-permute-start | bytes 294920 | tf_op jit(solution)/shard_map/ppermute | solution.py:20
  78.2 5.8 %collective-permute-start.13 = (bf16[48,8,128]{2,0,1:T(8,128)(2,1)}, bf16[48,8,128]{2,0,1:T(8,128)(2,1)}, u32[]{:S(2)}, u32[]{:S(2)}) collective-permute-start(bf16[48,8,128]{2,0,1:T(8,128)(2,1)} %get-tuple-element.42), channel_id=1, source_target_pairs={{8,0},{16,8},{24,16},{32,24},{40,32},{48,40},{56,48},{64,56},{72,6... | collective-permute-start | bytes 294920 | tf_op jit(solution)/shard_map/ppermute | solution.py:21
  84.0 0.9 fusion.14
  84.8 0.9 fusion.20
  85.8 0.9 fusion.19
  86.6 0.9 fusion.18
  87.5 0.9 fusion.17
  88.4 0.9 fusion.16
  89.3 0.9 fusion.13
  90.2 0.9 fusion.15
  91.1 1.1 reshape_reshape.3
  92.8 38.5 %shard_map.75 = f32[180,128]{1,0:T(8,128)} custom-call(f32[180,128]{1,0:T(8,128)} %maximum_bitcast_fusion.x_ref), custom_call_target="tpu_custom_call" | custom-call | tf_op jit(solution)/shard_map/pallas_call | solution.py:63
  131.3 0.9 slice_multiply_fusion
  136.3 1.0 reshape.79
  138.0 1.0 reshape.78
  139.1 8.9 %collective-permute-start.10 = (bf16[48,1024]{1,0:T(8,128)(2,1)}, bf16[48,1024]{1,0:T(8,128)(2,1)S(1)}, u32[]{:S(2)}, u32[]{:S(2)}) collective-permute-start(bf16[48,1024]{1,0:T(8,128)(2,1)} %reshape.78), channel_id=1, source_target_pairs={{0,16},{1,48},{2,80},{3,112},{4,144},{5,176},{6,208},{7,240},{8,24... | collective-permute-start | bytes 294920 | tf_op jit(solution)/shard_map/ppermute | solution.py:94
  148.7 1.1 reshape.77
  149.8 7.8 %collective-permute-start.9 = (bf16[48,1024]{1,0:T(8,128)(2,1)}, bf16[48,1024]{1,0:T(8,128)(2,1)S(1)}, u32[]{:S(2)}, u32[]{:S(2)}) collective-permute-start(bf16[48,1024]{1,0:T(8,128)(2,1)} %reshape.77), channel_id=1, source_target_pairs={{0,24},{1,56},{2,88},{3,120},{4,152},{5,184},{6,216},{7,248},{8,0}... | collective-permute-start | bytes 294920 | tf_op jit(solution)/shard_map/ppermute | solution.py:94
  158.3 1.0 reshape.76
  159.3 1.9 collective-permute-start.8
  161.2 1.0 pad_maximum_fusion.3
  162.5 1.1 copy.157
  163.6 1.2 copy.161
  164.8 2.2 %collective-permute-start.15 = (bf16[48,48,8]{1,2,0:T(8,128)(2,1)}, bf16[48,48,8]{1,2,0:T(8,128)(2,1)}, u32[]{:S(2)}, u32[]{:S(2)}) collective-permute-start(bf16[48,48,8]{1,2,0:T(8,128)(2,1)} %copy.161), channel_id=1, source_target_pairs={{0,1},{1,2},{2,3},{3,4},{4,5},{5,6},{6,7},{8,9},{9,10},{10,11},{11... | collective-permute-start | bytes 110600 | tf_op jit(solution)/shard_map/ppermute | solution.py:20
  167.0 6.0 %collective-permute-start.14 = (bf16[48,48,8]{1,2,0:T(8,128)(2,1)}, bf16[48,48,8]{1,2,0:T(8,128)(2,1)}, u32[]{:S(2)}, u32[]{:S(2)}) collective-permute-start(bf16[48,48,8]{1,2,0:T(8,128)(2,1)} %copy.157), channel_id=1, source_target_pairs={{1,0},{2,1},{3,2},{4,3},{5,4},{6,5},{7,6},{9,8},{10,9},{11,10},{12... | collective-permute-start | bytes 110600 | tf_op jit(solution)/shard_map/ppermute | solution.py:21
  173.4 9.4 %collective-permute-done.9 = bf16[48,1024]{1,0:T(8,128)(2,1)S(1)} collective-permute-done((bf16[48,1024]{1,0:T(8,128)(2,1)}, bf16[48,1024]{1,0:T(8,128)(2,1)S(1)}, u32[]{:S(2)}, u32[]{:S(2)}) %collective-permute-start.9) | collective-permute-done | bytes 98336 | tf_op jit(solution)/shard_map/ppermute | solution.py:94
  183.4 1.9 fusion.25
  185.6 1.5 copy.155
  187.1 1.5 add_convert_fusion
  188.6 2.0 %fusion.46 = f32[32,128,48]{1,2,0:T(8,128)} fusion(bf16[48,8,128]{2,0,1:T(8,128)(2,1)} %collective-permute-done.13, bf16[48,32,128]{2,0,1:T(8,128)(2,1)S(1)} %fusion.8, bf16[3,3,48,48]{3,2,1,0:T(8,128)(2,1)S(1)} %copy-done.10), kind=kOutput, calls=%fused_computation.101 | convolution fusion | flops 19857408 | bytes 1290240 | tf_op jit(solution)/shard_map/io,ohw->ihw/dot_general | solution.py:154
  190.6 1.1 fusion.50
  191.8 0.8 copy.170
  192.6 2.2 %copy.158 = bf16[48,48,8]{2,0,1:T(8,128)(2,1)} copy(bf16[48,48,8]{1,2,0:T(8,128)(2,1)} %collective-permute-done.14) | data formatting | bytes 73728 | tf_op jit(solution)/shard_map/ppermute | solution.py:21
  194.8 2.1 %copy.162 = bf16[48,48,8]{2,0,1:T(8,128)(2,1)} copy(bf16[48,48,8]{1,2,0:T(8,128)(2,1)} %collective-permute-done.15) | data formatting | bytes 73728 | tf_op jit(solution)/shard_map/ppermute | solution.py:20
  196.9 2.1 %pad_maximum_fusion.1 = (bf16[48,48,136]{2,0,1:T(8,128)(2,1)S(1)}, bf16[48,48,136]{2,0,1:T(8,128)(2,1)S(1)}) fusion(bf16[48,48,8]{2,0,1:T(8,128)(2,1)} %copy.158, bf16[48,8,128]{2,0,1:T(8,128)(2,1)} %collective-permute-done.13, bf16[48,32,128]{2,0,1:T(8,128)(2,1)S(1)} %fusion.8, bf16[48,8,128]{2,0,1:T(8,128)(2,1)} %collective-permute-done.12, ...), kind=kLoop, calls=%fused_computation.50 | loop fusion | flops 5013504 | bytes 1916928 | tf_op jit(solution)/shard_map/concatenate | solution.py:22
  199.3 0.9 copy-done.7
  202.2 0.8 copy.171
  (84 shorter events, 22.4 us)
Async XLA Ops:
  0.6 72.5 %copy-start = (bf16[48,48]{1,0:T(8,128)(2,1)S(1)}, bf16[48,48]{1,0:T(8,128)(2,1)}, u32[]{:S(2)}) copy-start(bf16[48,48]{1,0:T(8,128)(2,1)} %param.8) | copy-start | bytes 13828
  0.6 11.3 %copy-start.3 = (bf16[48,32,128]{2,1,0:T(8,128)(2,1)S(1)}, bf16[48,32,128]{2,1,0:T(8,128)(2,1)}, u32[]{:S(2)}) copy-start(bf16[48,32,128]{2,1,0:T(8,128)(2,1)} %param.9) | copy-start | bytes 1179652
  2.5 28.8 %collective-permute-start = (bf16[48,8,128]{2,0,1:T(8,128)(2,1)}, bf16[48,8,128]{2,0,1:T(8,128)(2,1)S(1)}, u32[]{:S(2)}, u32[]{:S(2)}) collective-permute-start(bf16[48,8,128]{2,0,1:T(8,128)(2,1)} %get-tuple-element.43), channel_id=1, source_target_pairs={{0,8},{8,16},{16,24},{24,32},{32,40},{40,48},{48,56},{56,64},{64,7... | collective-permute-start | bytes 294920 | tf_op jit(solution)/shard_map/ppermute | solution.py:20
  4.4 28.8 %collective-permute-start.1 = (bf16[48,8,128]{2,0,1:T(8,128)(2,1)}, bf16[48,8,128]{2,0,1:T(8,128)(2,1)S(1)}, u32[]{:S(2)}, u32[]{:S(2)}) collective-permute-start(bf16[48,8,128]{2,0,1:T(8,128)(2,1)} %get-tuple-element.44), channel_id=1, source_target_pairs={{8,0},{16,8},{24,16},{32,24},{40,32},{48,40},{56,48},{64,56},{72,6... | collective-permute-start | bytes 294920 | tf_op jit(solution)/shard_map/ppermute | solution.py:21
  15.0 22.8 %collective-permute-start.7 = (bf16[48,1024]{1,0:T(8,128)(2,1)}, bf16[48,1024]{1,0:T(8,128)(2,1)S(1)}, u32[]{:S(2)}, u32[]{:S(2)}) collective-permute-start(bf16[48,1024]{1,0:T(8,128)(2,1)} %reshape.71), channel_id=1, source_target_pairs={{0,8},{1,40},{2,72},{3,104},{4,136},{5,168},{6,200},{7,232},{8,16}... | collective-permute-start | bytes 294920 | tf_op jit(solution)/shard_map/ppermute | solution.py:94
  18.6 25.9 %collective-permute-start.6 = (bf16[48,1024]{1,0:T(8,128)(2,1)}, bf16[48,1024]{1,0:T(8,128)(2,1)S(1)}, u32[]{:S(2)}, u32[]{:S(2)}) collective-permute-start(bf16[48,1024]{1,0:T(8,128)(2,1)} %reshape.70), channel_id=1, source_target_pairs={{0,16},{1,48},{2,80},{3,112},{4,144},{5,176},{6,208},{7,240},{8,24... | collective-permute-start | bytes 294920 | tf_op jit(solution)/shard_map/ppermute | solution.py:94
  23.4 27.6 %collective-permute-start.5 = (bf16[48,1024]{1,0:T(8,128)(2,1)}, bf16[48,1024]{1,0:T(8,128)(2,1)}, u32[]{:S(2)}, u32[]{:S(2)}) collective-permute-start(bf16[48,1024]{1,0:T(8,128)(2,1)} %reshape.69), channel_id=1, source_target_pairs={{0,24},{1,56},{2,88},{3,120},{4,152},{5,184},{6,216},{7,248},{8,0}... | collective-permute-start | bytes 294920 | tf_op jit(solution)/shard_map/ppermute | solution.py:94
  31.4 24.1 %collective-permute-start.4 = (bf16[48,1024]{1,0:T(8,128)(2,1)}, bf16[48,1024]{1,0:T(8,128)(2,1)S(1)}, u32[]{:S(2)}, u32[]{:S(2)}) collective-permute-start(bf16[48,1024]{1,0:T(8,128)(2,1)} %reshape.68), channel_id=1, source_target_pairs={{0,0},{1,32},{2,64},{3,96},{4,128},{5,160},{6,192},{7,224},{8,8},{... | collective-permute-start | bytes 294920 | tf_op jit(solution)/shard_map/ppermute | solution.py:94
  35.9 27.3 %collective-permute-start.3 = (bf16[48,48,8]{1,2,0:T(8,128)(2,1)}, bf16[48,48,8]{1,2,0:T(8,128)(2,1)}, u32[]{:S(2)}, u32[]{:S(2)}) collective-permute-start(bf16[48,48,8]{1,2,0:T(8,128)(2,1)} %copy.125), channel_id=1, source_target_pairs={{1,0},{2,1},{3,2},{4,3},{5,4},{6,5},{7,6},{9,8},{10,9},{11,10},{12... | collective-permute-start | bytes 110600 | tf_op jit(solution)/shard_map/ppermute | solution.py:21
  37.8 23.2 %collective-permute-start.2 = (bf16[48,48,8]{1,2,0:T(8,128)(2,1)}, bf16[48,48,8]{1,2,0:T(8,128)(2,1)}, u32[]{:S(2)}, u32[]{:S(2)}) collective-permute-start(bf16[48,48,8]{1,2,0:T(8,128)(2,1)} %copy.121), channel_id=1, source_target_pairs={{0,1},{1,2},{2,3},{3,4},{4,5},{5,6},{6,7},{8,9},{9,10},{10,11},{11... | collective-permute-start | bytes 110600 | tf_op jit(solution)/shard_map/ppermute | solution.py:20
  57.5 0.9 copy-start.9
  67.4 7.8 %copy-start.4 = (bf16[48,48,136]{2,0,1:T(8,128)(2,1)}, bf16[48,48,136]{2,0,1:T(8,128)(2,1)S(1)}, u32[]{:S(2)}) copy-start(bf16[48,48,136]{2,0,1:T(8,128)(2,1)S(1)} %get-tuple-element.37) | copy-start | bytes 1880068
  67.4 1.6 copy-start.8
  69.6 1.0 copy-start.2
  71.6 1.1 copy-start.1
  76.2 9.6 %copy-start.5 = (bf16[48,48,136]{2,0,1:T(8,128)(2,1)S(1)}, bf16[48,48,136]{2,0,1:T(8,128)(2,1)}, u32[]{:S(2)}) copy-start(bf16[48,48,136]{2,0,1:T(8,128)(2,1)} %copy-done.4) | copy-start | bytes 1880068
  76.2 83.1 %collective-permute-start.12 = (bf16[48,8,128]{2,0,1:T(8,128)(2,1)}, bf16[48,8,128]{2,0,1:T(8,128)(2,1)}, u32[]{:S(2)}, u32[]{:S(2)}) collective-permute-start(bf16[48,8,128]{2,0,1:T(8,128)(2,1)} %get-tuple-element.41), channel_id=1, source_target_pairs={{0,8},{8,16},{16,24},{24,32},{32,40},{40,48},{48,56},{56,64},{64,7... | collective-permute-start | bytes 294920 | tf_op jit(solution)/shard_map/ppermute | solution.py:20
  78.2 83.0 %collective-permute-start.13 = (bf16[48,8,128]{2,0,1:T(8,128)(2,1)}, bf16[48,8,128]{2,0,1:T(8,128)(2,1)}, u32[]{:S(2)}, u32[]{:S(2)}) collective-permute-start(bf16[48,8,128]{2,0,1:T(8,128)(2,1)} %get-tuple-element.42), channel_id=1, source_target_pairs={{8,0},{16,8},{24,16},{32,24},{40,32},{48,40},{56,48},{64,56},{72,6... | collective-permute-start | bytes 294920 | tf_op jit(solution)/shard_map/ppermute | solution.py:21
  89.3 42.9 %copy-start.6 = (bf16[48,32,128]{2,0,1:T(8,128)(2,1)S(1)}, bf16[48,32,128]{2,0,1:T(8,128)(2,1)}, u32[]{:S(2)}) copy-start(bf16[48,32,128]{2,0,1:T(8,128)(2,1)} %fusion.12) | copy-start | bytes 1179652
  137.3 29.7 %collective-permute-start.11 = (bf16[48,1024]{1,0:T(8,128)(2,1)}, bf16[48,1024]{1,0:T(8,128)(2,1)S(1)}, u32[]{:S(2)}, u32[]{:S(2)}) collective-permute-start(bf16[48,1024]{1,0:T(8,128)(2,1)} %reshape.79), channel_id=1, source_target_pairs={{0,8},{1,40},{2,72},{3,104},{4,136},{5,168},{6,200},{7,232},{8,16}... | collective-permute-start | bytes 294920 | tf_op jit(solution)/shard_map/ppermute | solution.py:94
  139.1 34.1 %collective-permute-start.10 = (bf16[48,1024]{1,0:T(8,128)(2,1)}, bf16[48,1024]{1,0:T(8,128)(2,1)S(1)}, u32[]{:S(2)}, u32[]{:S(2)}) collective-permute-start(bf16[48,1024]{1,0:T(8,128)(2,1)} %reshape.78), channel_id=1, source_target_pairs={{0,16},{1,48},{2,80},{3,112},{4,144},{5,176},{6,208},{7,240},{8,24... | collective-permute-start | bytes 294920 | tf_op jit(solution)/shard_map/ppermute | solution.py:94
  149.8 33.1 %collective-permute-start.9 = (bf16[48,1024]{1,0:T(8,128)(2,1)}, bf16[48,1024]{1,0:T(8,128)(2,1)S(1)}, u32[]{:S(2)}, u32[]{:S(2)}) collective-permute-start(bf16[48,1024]{1,0:T(8,128)(2,1)} %reshape.77), channel_id=1, source_target_pairs={{0,24},{1,56},{2,88},{3,120},{4,152},{5,184},{6,216},{7,248},{8,0}... | collective-permute-start | bytes 294920 | tf_op jit(solution)/shard_map/ppermute | solution.py:94
  159.3 23.9 %collective-permute-start.8 = (bf16[48,1024]{1,0:T(8,128)(2,1)}, bf16[48,1024]{1,0:T(8,128)(2,1)S(1)}, u32[]{:S(2)}, u32[]{:S(2)}) collective-permute-start(bf16[48,1024]{1,0:T(8,128)(2,1)} %reshape.76), channel_id=1, source_target_pairs={{0,0},{1,32},{2,64},{3,96},{4,128},{5,160},{6,192},{7,224},{8,8},{... | collective-permute-start | bytes 294920 | tf_op jit(solution)/shard_map/ppermute | solution.py:94
  164.8 30.0 %collective-permute-start.15 = (bf16[48,48,8]{1,2,0:T(8,128)(2,1)}, bf16[48,48,8]{1,2,0:T(8,128)(2,1)}, u32[]{:S(2)}, u32[]{:S(2)}) collective-permute-start(bf16[48,48,8]{1,2,0:T(8,128)(2,1)} %copy.161), channel_id=1, source_target_pairs={{0,1},{1,2},{2,3},{3,4},{4,5},{5,6},{6,7},{8,9},{9,10},{10,11},{11... | collective-permute-start | bytes 110600 | tf_op jit(solution)/shard_map/ppermute | solution.py:20
  167.0 25.7 %collective-permute-start.14 = (bf16[48,48,8]{1,2,0:T(8,128)(2,1)}, bf16[48,48,8]{1,2,0:T(8,128)(2,1)}, u32[]{:S(2)}, u32[]{:S(2)}) collective-permute-start(bf16[48,48,8]{1,2,0:T(8,128)(2,1)} %copy.157), channel_id=1, source_target_pairs={{1,0},{2,1},{3,2},{4,3},{5,4},{6,5},{7,6},{9,8},{10,9},{11,10},{12... | collective-permute-start | bytes 110600 | tf_op jit(solution)/shard_map/ppermute | solution.py:21
  187.1 1.5 copy-start.10
  199.1 1.1 copy-start.7

commit v3 on v0

--- a/solution.py
+++ b/solution.py
@@ -136,9 +136,6 @@
             )
     local_kernel = jnp.stack(tap_grads).reshape(3, 3, chans, chans)
     flat = jnp.concatenate([local_kernel.reshape(-1), local_mixing.reshape(-1)])
-    sums = all_sum(flat.reshape(-1, 128)).reshape(-1)
-    grad_kernel = sums[: 9 * chans * chans].reshape(3, 3, chans, chans)
-    grad_mixing = sums[9 * chans * chans :].reshape(chans, chans)
     grad_padded = with_halo(grad_before, (("row", 1), ("col", 2)), DILATION)
     grad_active = jnp.zeros((chans, rows, cols), jnp.float32)
     for row_tap in range(3):
@@ -154,6 +151,10 @@
                 "io,ohw->ihw", kernel[row_tap, col_tap], piece, preferred_element_type=jnp.float32
             )
     grad_maps = (grad_wide + jnp.where(maps > 0, grad_active, 0.0)).astype(jnp.bfloat16)
+    flat, output, grad_maps = lax.optimization_barrier((flat, output, grad_maps))
+    sums = all_sum(flat.reshape(-1, 128)).reshape(-1)
+    grad_kernel = sums[: 9 * chans * chans].reshape(3, 3, chans, chans)
+    grad_mixing = sums[9 * chans * chans :].reshape(chans, chans)
     return (output, grad_maps, grad_kernel / map_bins, grad_mixing / map_bins)
 
 

time: 199 us -> 204 us (1.025); the launches traced: 197 us -> 200 us
  Pallas kernels: 45.5 us -> 35.8 us
  matrix products: 16.4 us -> 23.1 us
  waiting for transfers between devices: 23 us -> 27.4 us
  starting transfers between devices: 66.9 us -> 70.3 us
    pallas_call x1, Pallas kernels: 45.5 us -> 35.8 us  [all_sum(): pl.pallas_call(functools.partial(sum_kernel, strides), out_shape=jax.Shap...]
    dot_general x9, matrix products: 3.37 us -> 10.9 us  [shards(): jnp.einsum('ihw,ohw->io', piece, grad_before, preferred_element_type=jnp....]
    ppermute x4, starting transfers between devices: 13.4 us -> 20 us  [with_halo(): before = lax.ppermute(last, axis, up)]
    ppermute x4, waiting for transfers between devices: 0.06 us -> 4.45 us  [with_halo(): after = lax.ppermute(initial, axis, down)]
    ppermute x4, starting transfers between devices: 19.8 us -> 16.5 us  [with_halo(): after = lax.ppermute(initial, axis, down)]
    unnamed x33 -> x39, local copies, waits for them, and re-layouts: 4.72 us -> 3.85 us
  transfers between devices with their start and end apart: 16 -> 16, of which waited for: 4 -> 4; matrix products, arithmetic and copies ran while one was open for 19% -> 18% of each run, Pallas kernels for 23% -> 0%
where the time goes in v3:
time: 204 us; the launch traced here: 200 us
  starting transfers between devices  70.3 us (34%)
  Pallas kernels  35.8 us (18%)
  waiting for transfers between devices  27.4 us (13%)
  local copies, waits for them, and re-layouts  26.9 us (13%)
  matrix products  23.1 us (11%)
  other arithmetic  15.2 us (7%)
    pallas_call x1, Pallas kernels, all_sum(): pl.pallas_call(functools.partial(sum_kernel, strides), out_shape=jax.Shap...  35.8 us
    ppermute x8, starting transfers between devices, mirror_tile(): lax.ppermute(piece, ('row', 'col'), pairs).reshape(chans, rows, rows)  33.8 us
    ppermute x8, waiting for transfers between devices, mirror_tile(): lax.ppermute(piece, ('row', 'col'), pairs).reshape(chans, rows, rows)  21 us
    ppermute x4, starting transfers between devices, with_halo(): before = lax.ppermute(last, axis, up)  20 us
    ppermute x4, starting transfers between devices, with_halo(): after = lax.ppermute(initial, axis, down)  16.5 us
    dot_general x9, matrix products, shards(): jnp.einsum('ihw,ohw->io', piece, grad_before, preferred_element_type=jnp....  10.9 us
    transpose x10, local copies, waits for them, and re-layouts, mirror_tile(): piece = jnp.swapaxes(pieces[:, :, k, :], 1, 2).reshape(chans, rows * rows)  5.89 us
    concatenate x1, other arithmetic, mirror_tile(): return jnp.roll(slots, turn, axis=2).reshape(chans, rows, cols)  4.54 us
  transfers between devices with their start and end apart: 16, of which 4 were waited for; matrix products, arithmetic and copies ran while one was open for 18% of the time, Pallas kernels for 0%

profile of v3, /device:TPU:6, one launch (start us, length us, event | category | flops | bytes accessed | tf_op | source)
XLA Modules:
  0.0 200.1 jit_solution(10181196784167248507)
XLA Ops:
  0.7 1.2 copy_maximum_fusion
  1.9 1.9 collective-permute-start
  3.8 7.5 %collective-permute-start.1 = (bf16[48,8,128]{2,0,1:T(8,128)(2,1)S(1)}, bf16[48,8,128]{2,0,1:T(8,128)(2,1)S(1)}, u32[]{:S(2)}, u32[]{:S(2)}) collective-permute-start(bf16[48,8,128]{2,0,1:T(8,128)(2,1)S(1)} %get-tuple-element.46), channel_id=1, source_target_pairs={{8,0},{16,8},{24,16},{32,24},{40,32},{48,40},{56,48},{64,56},{72,6... | collective-permute-start | bytes 294920 | tf_op jit(solution)/shard_map/ppermute | solution.py:21
  12.6 0.7 copy.138
  13.7 2.0 collective-permute-start.7
  15.7 0.7 copy.137
  16.8 3.1 %collective-permute-start.6 = (bf16[48,1024]{1,0:T(8,128)(2,1)S(1)}, bf16[48,1024]{1,0:T(8,128)(2,1)S(1)}, u32[]{:S(2)}, u32[]{:S(2)}) collective-permute-start(bf16[48,1024]{1,0:T(8,128)(2,1)S(1)} %reshape.64), channel_id=1, source_target_pairs={{0,16},{1,48},{2,80},{3,112},{4,144},{5,176},{6,208},{7,240},{8,24... | collective-permute-start | bytes 294920 | tf_op jit(solution)/shard_map/ppermute | solution.py:94
  19.9 0.7 copy.136
  21.0 6.3 %collective-permute-start.5 = (bf16[48,1024]{1,0:T(8,128)(2,1)S(1)}, bf16[48,1024]{1,0:T(8,128)(2,1)S(1)}, u32[]{:S(2)}, u32[]{:S(2)}) collective-permute-start(bf16[48,1024]{1,0:T(8,128)(2,1)S(1)} %reshape.63), channel_id=1, source_target_pairs={{0,24},{1,56},{2,88},{3,120},{4,152},{5,184},{6,216},{7,248},{8,0}... | collective-permute-start | bytes 294920 | tf_op jit(solution)/shard_map/ppermute | solution.py:94
  27.3 0.7 copy.135
  29.8 1.9 collective-permute-start.3
  31.7 6.3 %collective-permute-start.2 = (bf16[48,48,8]{1,2,0:T(8,128)(2,1)S(1)}, bf16[48,48,8]{1,2,0:T(8,128)(2,1)S(1)}, u32[]{:S(2)}, u32[]{:S(2)}) collective-permute-start(bf16[48,48,8]{1,2,0:T(8,128)(2,1)S(1)} %copy.120), channel_id=1, source_target_pairs={{0,1},{1,2},{2,3},{3,4},{4,5},{5,6},{6,7},{8,9},{9,10},{10,11},{11... | collective-permute-start | bytes 110600 | tf_op jit(solution)/shard_map/ppermute | solution.py:20
  38.4 1.9 collective-permute-done.2
  40.3 8.1 %collective-permute-start.4 = (bf16[48,1024]{1,0:T(8,128)(2,1)S(1)}, bf16[48,1024]{1,0:T(8,128)(2,1)S(1)}, u32[]{:S(2)}, u32[]{:S(2)}) collective-permute-start(bf16[48,1024]{1,0:T(8,128)(2,1)S(1)} %reshape.62), channel_id=1, source_target_pairs={{0,0},{1,32},{2,64},{3,96},{4,128},{5,160},{6,192},{7,224},{8,8},{... | collective-permute-start | bytes 294920 | tf_op jit(solution)/shard_map/ppermute | solution.py:94
  48.9 1.4 copy.125
  50.3 0.8 maximum_maximum_fusion
  52.4 0.7 copy-done.1
  54.0 1.0 fusion.11
  55.1 1.3 fusion.12
  57.5 0.7 copy.150
  58.7 0.7 copy.149
  59.9 0.7 copy.148
  61.0 0.7 copy.147
  62.1 5.1 %collective-permute-start.10 = (bf16[48,1024]{1,0:T(8,128)(2,1)S(1)}, bf16[48,1024]{1,0:T(8,128)(2,1)S(1)}, u32[]{:S(2)}, u32[]{:S(2)}) collective-permute-start(bf16[48,1024]{1,0:T(8,128)(2,1)S(1)} %reshape.70), channel_id=1, source_target_pairs={{0,16},{1,48},{2,80},{3,112},{4,144},{5,176},{6,208},{7,240},{8,24... | collective-permute-start | bytes 294920 | tf_op jit(solution)/shard_map/ppermute | solution.py:94
  67.2 3.1 %collective-permute-start.9 = (bf16[48,1024]{1,0:T(8,128)(2,1)S(1)}, bf16[48,1024]{1,0:T(8,128)(2,1)S(1)}, u32[]{:S(2)}, u32[]{:S(2)}) collective-permute-start(bf16[48,1024]{1,0:T(8,128)(2,1)S(1)} %reshape.69), channel_id=1, source_target_pairs={{0,24},{1,56},{2,88},{3,120},{4,152},{5,184},{6,216},{7,248},{8,0}... | collective-permute-start | bytes 294920 | tf_op jit(solution)/shard_map/ppermute | solution.py:94
  70.4 6.0 %collective-permute-start.8 = (bf16[48,1024]{1,0:T(8,128)(2,1)S(1)}, bf16[48,1024]{1,0:T(8,128)(2,1)S(1)}, u32[]{:S(2)}, u32[]{:S(2)}) collective-permute-start(bf16[48,1024]{1,0:T(8,128)(2,1)S(1)} %reshape.68), channel_id=1, source_target_pairs={{0,0},{1,32},{2,64},{3,96},{4,128},{5,160},{6,192},{7,224},{8,8},{... | collective-permute-start | bytes 294920 | tf_op jit(solution)/shard_map/ppermute | solution.py:94
  77.5 18.1 %collective-permute-done.9 = bf16[48,1024]{1,0:T(8,128)(2,1)S(1)} collective-permute-done((bf16[48,1024]{1,0:T(8,128)(2,1)S(1)}, bf16[48,1024]{1,0:T(8,128)(2,1)S(1)}, u32[]{:S(2)}, u32[]{:S(2)}) %collective-permute-start.9) | collective-permute-done | bytes 98336 | tf_op jit(solution)/shard_map/ppermute | solution.py:94
  95.8 2.9 %collective-permute-done.8 = bf16[48,1024]{1,0:T(8,128)(2,1)S(1)} collective-permute-done((bf16[48,1024]{1,0:T(8,128)(2,1)S(1)}, bf16[48,1024]{1,0:T(8,128)(2,1)S(1)}, u32[]{:S(2)}, u32[]{:S(2)}) %collective-permute-start.8) | collective-permute-done | bytes 98336 | tf_op jit(solution)/shard_map/ppermute | solution.py:94
  98.9 4.5 %fusion.25 = (bf16[48,32,4,32]{0,3,2,1:T(8,128)(2,1)}, bf16[48,32,4,32]{0,3,2,1:T(8,128)(2,1)S(1)}) fusion(s32[]{:T(128)S(6)} %select_n.37, bf16[48,32,1,32]{0,3,2,1:T(8,128)(2,1)S(1)} %bitcast.231, bf16[48,32,1,32]{0,3,2,1:T(8,128)(2,1)S(1)} %bitcast.230, bf16[48,32,1,32]{0,3,2,1:T(8,128)(2,1)S(1)} %bitcast.229, bf16[48,32,1,32]{0,3,2,1:T(8,128)(2,1)S(1)} %bitcast.228, ...), kind=kLoop, calls=%fused_computation.74 | loop fusion | flops 2752512 | bytes 1572868 | tf_op jit(solution)/shard_map/jit(_roll_dynamic)/concatenate | solution.py:96
  104.3 1.6 convolution_bitcast_fusion.3
  105.9 1.4 fusion.8
  107.3 0.7 fusion.129
  108.0 1.8 fusion.21
  110.1 1.5 copy.155
  111.6 0.7 reshape.66
  112.3 2.9 %collective-permute-start.12 = (bf16[48,8,128]{2,0,1:T(8,128)(2,1)}, bf16[48,8,128]{2,0,1:T(8,128)(2,1)}, u32[]{:S(2)}, u32[]{:S(2)}) collective-permute-start(bf16[48,8,128]{2,0,1:T(8,128)(2,1)} %get-tuple-element.43), channel_id=1, source_target_pairs={{0,8},{8,16},{16,24},{24,32},{32,40},{40,48},{48,56},{56,64},{64,7... | collective-permute-start | bytes 294920 | tf_op jit(solution)/shard_map/ppermute | solution.py:20
  115.2 4.9 %collective-permute-start.13 = (bf16[48,8,128]{2,0,1:T(8,128)(2,1)}, bf16[48,8,128]{2,0,1:T(8,128)(2,1)}, u32[]{:S(2)}, u32[]{:S(2)}) collective-permute-start(bf16[48,8,128]{2,0,1:T(8,128)(2,1)} %get-tuple-element.44), channel_id=1, source_target_pairs={{8,0},{16,8},{24,16},{32,24},{40,32},{48,40},{56,48},{64,56},{72,6... | collective-permute-start | bytes 294920 | tf_op jit(solution)/shard_map/ppermute | solution.py:21
  120.1 0.9 fusion.14
  121.0 0.9 fusion.20
  121.9 1.8 fusion.19
  123.8 0.9 fusion.18
  124.6 0.9 fusion.17
  125.6 1.8 fusion.16
  127.4 0.9 fusion.13
  128.3 0.9 fusion.15
  129.2 1.1 reshape_reshape.3
  130.3 1.4 pad_maximum_fusion.4
  131.7 0.9 add_convert_fusion
  132.6 1.0 pad_maximum_fusion.3
  134.9 8.8 %collective-permute-start.15 = (bf16[48,48,8]{1,2,0:T(8,128)(2,1)S(1)}, bf16[48,48,8]{1,2,0:T(8,128)(2,1)S(1)}, u32[]{:S(2)}, u32[]{:S(2)}) collective-permute-start(bf16[48,48,8]{1,2,0:T(8,128)(2,1)S(1)} %copy.161), channel_id=1, source_target_pairs={{0,1},{1,2},{2,3},{3,4},{4,5},{5,6},{6,7},{8,9},{9,10},{10,11},{11... | collective-permute-start | bytes 110600 | tf_op jit(solution)/shard_map/ppermute | solution.py:20
  143.8 2.2 %collective-permute-start.14 = (bf16[48,48,8]{1,2,0:T(8,128)(2,1)S(1)}, bf16[48,48,8]{1,2,0:T(8,128)(2,1)S(1)}, u32[]{:S(2)}, u32[]{:S(2)}) collective-permute-start(bf16[48,48,8]{1,2,0:T(8,128)(2,1)S(1)} %copy.157), channel_id=1, source_target_pairs={{1,0},{2,1},{3,2},{4,3},{5,4},{6,5},{7,6},{9,8},{10,9},{11,10},{12... | collective-permute-start | bytes 110600 | tf_op jit(solution)/shard_map/ppermute | solution.py:21
  146.0 1.1 fusion.46
  147.1 1.1 fusion.50
  148.2 4.4 %collective-permute-done.14 = bf16[48,48,8]{1,2,0:T(8,128)(2,1)S(1)} collective-permute-done((bf16[48,48,8]{1,2,0:T(8,128)(2,1)S(1)}, bf16[48,48,8]{1,2,0:T(8,128)(2,1)S(1)}, u32[]{:S(2)}, u32[]{:S(2)}) %collective-permute-start.14) | collective-permute-done | bytes 36896 | tf_op jit(solution)/shard_map/ppermute | solution.py:21
  153.2 1.3 copy.162
  154.5 2.0 %pad_maximum_fusion.1 = (bf16[48,48,136]{2,0,1:T(8,128)(2,1)S(1)}, bf16[48,48,136]{2,0,1:T(8,128)(2,1)S(1)}) fusion(bf16[48,48,8]{2,0,1:T(8,128)(2,1)S(1)} %copy.158, bf16[48,8,128]{2,0,1:T(8,128)(2,1)} %collective-permute-done.13, bf16[48,32,128]{2,0,1:T(8,128)(2,1)S(1)} %fusion.8, bf16[48,8,128]{2,0,1:T(8,128)(2,1)} %collective-permute-done.12, ...), kind=kLoop, calls=%fused_computation.50 | loop fusion | flops 5013504 | bytes 1916928 | tf_op jit(solution)/shard_map/concatenate | solution.py:22
  158.2 0.7 copy-done.5
  159.5 35.8 %shard_map.75 = f32[180,128]{1,0:T(8,128)} custom-call(f32[180,128]{1,0:T(8,128)} %bitcast.232), custom_call_target="tpu_custom_call" | custom-call | tf_op jit(solution)/shard_map/pallas_call | solution.py:63
  195.3 0.7 slice_multiply_fusion.1
  196.0 0.9 slice_multiply_fusion
  196.9 0.8 copy.170
  197.8 0.7 div.21
  198.5 0.8 div.18
  199.3 0.8 copy.171
  (97 shorter events, 16.4 us)
Async XLA Ops:
  0.6 54.5 %copy-start = (bf16[48,48]{1,0:T(8,128)(2,1)S(1)}, bf16[48,48]{1,0:T(8,128)(2,1)}, u32[]{:S(2)}) copy-start(bf16[48,48]{1,0:T(8,128)(2,1)} %param.8) | copy-start | bytes 13828
  0.6 10.7 %copy-start.3 = (bf16[48,32,128]{2,1,0:T(8,128)(2,1)S(1)}, bf16[48,32,128]{2,1,0:T(8,128)(2,1)}, u32[]{:S(2)}) copy-start(bf16[48,32,128]{2,1,0:T(8,128)(2,1)} %param.9) | copy-start | bytes 1179652
  1.9 26.6 %collective-permute-start = (bf16[48,8,128]{2,0,1:T(8,128)(2,1)S(1)}, bf16[48,8,128]{2,0,1:T(8,128)(2,1)S(1)}, u32[]{:S(2)}, u32[]{:S(2)}) collective-permute-start(bf16[48,8,128]{2,0,1:T(8,128)(2,1)S(1)} %get-tuple-element.45), channel_id=1, source_target_pairs={{0,8},{8,16},{16,24},{24,32},{32,40},{40,48},{48,56},{56,64},{64,7... | collective-permute-start | bytes 294920 | tf_op jit(solution)/shard_map/ppermute | solution.py:20
  3.8 24.6 %collective-permute-start.1 = (bf16[48,8,128]{2,0,1:T(8,128)(2,1)S(1)}, bf16[48,8,128]{2,0,1:T(8,128)(2,1)S(1)}, u32[]{:S(2)}, u32[]{:S(2)}) collective-permute-start(bf16[48,8,128]{2,0,1:T(8,128)(2,1)S(1)} %get-tuple-element.46), channel_id=1, source_target_pairs={{8,0},{16,8},{24,16},{32,24},{40,32},{48,40},{56,48},{64,56},{72,6... | collective-permute-start | bytes 294920 | tf_op jit(solution)/shard_map/ppermute | solution.py:21
  13.7 48.4 %collective-permute-start.7 = (bf16[48,1024]{1,0:T(8,128)(2,1)S(1)}, bf16[48,1024]{1,0:T(8,128)(2,1)S(1)}, u32[]{:S(2)}, u32[]{:S(2)}) collective-permute-start(bf16[48,1024]{1,0:T(8,128)(2,1)S(1)} %reshape.65), channel_id=1, source_target_pairs={{0,8},{1,40},{2,72},{3,104},{4,136},{5,168},{6,200},{7,232},{8,16}... | collective-permute-start | bytes 294920 | tf_op jit(solution)/shard_map/ppermute | solution.py:94
  16.8 50.4 %collective-permute-start.6 = (bf16[48,1024]{1,0:T(8,128)(2,1)S(1)}, bf16[48,1024]{1,0:T(8,128)(2,1)S(1)}, u32[]{:S(2)}, u32[]{:S(2)}) collective-permute-start(bf16[48,1024]{1,0:T(8,128)(2,1)S(1)} %reshape.64), channel_id=1, source_target_pairs={{0,16},{1,48},{2,80},{3,112},{4,144},{5,176},{6,208},{7,240},{8,24... | collective-permute-start | bytes 294920 | tf_op jit(solution)/shard_map/ppermute | solution.py:94
  21.0 49.4 %collective-permute-start.5 = (bf16[48,1024]{1,0:T(8,128)(2,1)S(1)}, bf16[48,1024]{1,0:T(8,128)(2,1)S(1)}, u32[]{:S(2)}, u32[]{:S(2)}) collective-permute-start(bf16[48,1024]{1,0:T(8,128)(2,1)S(1)} %reshape.63), channel_id=1, source_target_pairs={{0,24},{1,56},{2,88},{3,120},{4,152},{5,184},{6,216},{7,248},{8,0}... | collective-permute-start | bytes 294920 | tf_op jit(solution)/shard_map/ppermute | solution.py:94
  28.4 25.6 %copy-start.14 = (bf16[48,8,128]{2,0,1:T(8,128)(2,1)}, bf16[48,8,128]{2,0,1:T(8,128)(2,1)S(1)}, u32[]{:S(2)}) copy-start(bf16[48,8,128]{2,0,1:T(8,128)(2,1)S(1)} %collective-permute-done.1) | copy-start | bytes 294916
  28.8 9.3 %copy-start.16 = (bf16[3,3,48,48]{3,2,1,0:T(8,128)(2,1)S(1)}, bf16[3,3,48,48]{3,2,1,0:T(8,128)(2,1)}, u32[]{:S(2)}) copy-start(bf16[3,3,48,48]{3,2,1,0:T(8,128)(2,1)} %param.7) | copy-start | bytes 124420
  29.8 19.0 %collective-permute-start.3 = (bf16[48,48,8]{1,2,0:T(8,128)(2,1)S(1)}, bf16[48,48,8]{1,2,0:T(8,128)(2,1)}, u32[]{:S(2)}, u32[]{:S(2)}) collective-permute-start(bf16[48,48,8]{1,2,0:T(8,128)(2,1)S(1)} %copy.124), channel_id=1, source_target_pairs={{1,0},{2,1},{3,2},{4,3},{5,4},{6,5},{7,6},{9,8},{10,9},{11,10},{12... | collective-permute-start | bytes 110600 | tf_op jit(solution)/shard_map/ppermute | solution.py:21
  31.7 8.5 %collective-permute-start.2 = (bf16[48,48,8]{1,2,0:T(8,128)(2,1)S(1)}, bf16[48,48,8]{1,2,0:T(8,128)(2,1)S(1)}, u32[]{:S(2)}, u32[]{:S(2)}) collective-permute-start(bf16[48,48,8]{1,2,0:T(8,128)(2,1)S(1)} %copy.120), channel_id=1, source_target_pairs={{0,1},{1,2},{2,3},{3,4},{4,5},{5,6},{6,7},{8,9},{9,10},{10,11},{11... | collective-permute-start | bytes 110600 | tf_op jit(solution)/shard_map/ppermute | solution.py:20
  40.3 36.7 %collective-permute-start.4 = (bf16[48,1024]{1,0:T(8,128)(2,1)S(1)}, bf16[48,1024]{1,0:T(8,128)(2,1)S(1)}, u32[]{:S(2)}, u32[]{:S(2)}) collective-permute-start(bf16[48,1024]{1,0:T(8,128)(2,1)S(1)} %reshape.62), channel_id=1, source_target_pairs={{0,0},{1,32},{2,64},{3,96},{4,128},{5,160},{6,192},{7,224},{8,8},{... | collective-permute-start | bytes 294920 | tf_op jit(solution)/shard_map/ppermute | solution.py:94
  51.1 2.3 %copy-start.6 = (bf16[48,48,136]{2,0,1:T(8,128)(2,1)}, bf16[48,48,136]{2,0,1:T(8,128)(2,1)S(1)}, u32[]{:S(2)}) copy-start(bf16[48,48,136]{2,0,1:T(8,128)(2,1)S(1)} %get-tuple-element.40) | copy-start | bytes 1880068
  51.1 2.6 %copy-start.8 = (bf16[48,48,136]{2,0,1:T(8,128)(2,1)}, bf16[48,48,136]{2,0,1:T(8,128)(2,1)S(1)}, u32[]{:S(2)}) copy-start(bf16[48,48,136]{2,0,1:T(8,128)(2,1)S(1)} %get-tuple-element.39) | copy-start | bytes 1880068
  52.1 1.0 copy-start.1
  56.4 1.0 copy-start.10
  58.7 18.5 %collective-permute-start.11 = (bf16[48,1024]{1,0:T(8,128)(2,1)S(1)}, bf16[48,1024]{1,0:T(8,128)(2,1)S(1)}, u32[]{:S(2)}, u32[]{:S(2)}) collective-permute-start(bf16[48,1024]{1,0:T(8,128)(2,1)S(1)} %reshape.71), channel_id=1, source_target_pairs={{0,8},{1,40},{2,72},{3,104},{4,136},{5,168},{6,200},{7,232},{8,16}... | collective-permute-start | bytes 294920 | tf_op jit(solution)/shard_map/ppermute | solution.py:94
  62.1 15.2 %collective-permute-start.10 = (bf16[48,1024]{1,0:T(8,128)(2,1)S(1)}, bf16[48,1024]{1,0:T(8,128)(2,1)S(1)}, u32[]{:S(2)}, u32[]{:S(2)}) collective-permute-start(bf16[48,1024]{1,0:T(8,128)(2,1)S(1)} %reshape.70), channel_id=1, source_target_pairs={{0,16},{1,48},{2,80},{3,112},{4,144},{5,176},{6,208},{7,240},{8,24... | collective-permute-start | bytes 294920 | tf_op jit(solution)/shard_map/ppermute | solution.py:94
  67.2 28.4 %collective-permute-start.9 = (bf16[48,1024]{1,0:T(8,128)(2,1)S(1)}, bf16[48,1024]{1,0:T(8,128)(2,1)S(1)}, u32[]{:S(2)}, u32[]{:S(2)}) collective-permute-start(bf16[48,1024]{1,0:T(8,128)(2,1)S(1)} %reshape.69), channel_id=1, source_target_pairs={{0,24},{1,56},{2,88},{3,120},{4,152},{5,184},{6,216},{7,248},{8,0}... | collective-permute-start | bytes 294920 | tf_op jit(solution)/shard_map/ppermute | solution.py:94
  70.4 28.3 %collective-permute-start.8 = (bf16[48,1024]{1,0:T(8,128)(2,1)S(1)}, bf16[48,1024]{1,0:T(8,128)(2,1)S(1)}, u32[]{:S(2)}, u32[]{:S(2)}) collective-permute-start(bf16[48,1024]{1,0:T(8,128)(2,1)S(1)} %reshape.68), channel_id=1, source_target_pairs={{0,0},{1,32},{2,64},{3,96},{4,128},{5,160},{6,192},{7,224},{8,8},{... | collective-permute-start | bytes 294920 | tf_op jit(solution)/shard_map/ppermute | solution.py:94
  104.3 1.6 copy-start.4
  105.9 3.9 %copy-start.9 = (bf16[48,32,4,32]{0,3,2,1:T(8,128)(2,1)S(1)}, bf16[48,32,4,32]{0,3,2,1:T(8,128)(2,1)}, u32[]{:S(2)}) copy-start(bf16[48,32,4,32]{0,3,2,1:T(8,128)(2,1)} %get-tuple-element.47) | copy-start | bytes 1179652
  111.6 9.4 %copy-start.7 = (bf16[48,48,136]{2,0,1:T(8,128)(2,1)S(1)}, bf16[48,48,136]{2,0,1:T(8,128)(2,1)}, u32[]{:S(2)}) copy-start(bf16[48,48,136]{2,0,1:T(8,128)(2,1)} %copy-done.6) | copy-start | bytes 1880068
  112.3 20.3 %collective-permute-start.12 = (bf16[48,8,128]{2,0,1:T(8,128)(2,1)}, bf16[48,8,128]{2,0,1:T(8,128)(2,1)}, u32[]{:S(2)}, u32[]{:S(2)}) collective-permute-start(bf16[48,8,128]{2,0,1:T(8,128)(2,1)} %get-tuple-element.43), channel_id=1, source_target_pairs={{0,8},{8,16},{16,24},{24,32},{32,40},{40,48},{48,56},{56,64},{64,7... | collective-permute-start | bytes 294920 | tf_op jit(solution)/shard_map/ppermute | solution.py:20
  115.2 8.6 %copy-start.2 = (bf16[48,32,128]{2,1,0:T(8,128)(2,1)S(1)}, bf16[48,32,128]{2,1,0:T(8,128)(2,1)}, u32[]{:S(2)}) copy-start(bf16[48,32,128]{2,1,0:T(8,128)(2,1)} %param.6) | copy-start | bytes 1179652
  115.2 17.4 %collective-permute-start.13 = (bf16[48,8,128]{2,0,1:T(8,128)(2,1)}, bf16[48,8,128]{2,0,1:T(8,128)(2,1)}, u32[]{:S(2)}, u32[]{:S(2)}) collective-permute-start(bf16[48,8,128]{2,0,1:T(8,128)(2,1)} %get-tuple-element.44), channel_id=1, source_target_pairs={{8,0},{16,8},{24,16},{32,24},{40,32},{48,40},{56,48},{64,56},{72,6... | collective-permute-start | bytes 294920 | tf_op jit(solution)/shard_map/ppermute | solution.py:21
  123.8 3.7 %copy-start.15 = (bf16[48,8,128]{2,0,1:T(8,128)(2,1)S(1)}, bf16[48,8,128]{2,0,1:T(8,128)(2,1)}, u32[]{:S(2)}) copy-start(bf16[48,8,128]{2,0,1:T(8,128)(2,1)} %copy-done.14) | copy-start | bytes 294916
  127.4 4.2 %copy-start.11 = (bf16[48,32,128]{2,0,1:T(8,128)(2,1)S(1)}, bf16[48,32,128]{2,0,1:T(8,128)(2,1)}, u32[]{:S(2)}) copy-start(bf16[48,32,128]{2,0,1:T(8,128)(2,1)} %copy-done.10) | copy-start | bytes 1179652
  127.4 4.2 %copy-start.12 = (f32[48,32,128]{2,0,1:T(8,128)S(1)}, f32[48,32,128]{2,0,1:T(8,128)}, u32[]{:S(2)}) copy-start(f32[48,32,128]{2,0,1:T(8,128)} %copy.155) | copy-start | bytes 2359300
  133.9 12.1 %copy-start.17 = (bf16[3,3,48,48]{3,2,1,0:T(8,128)(2,1)S(1)}, bf16[3,3,48,48]{3,2,1,0:T(8,128)(2,1)}, u32[]{:S(2)}) copy-start(bf16[3,3,48,48]{3,2,1,0:T(8,128)(2,1)} %param.7) | copy-start | bytes 124420
  134.9 18.3 %collective-permute-start.15 = (bf16[48,48,8]{1,2,0:T(8,128)(2,1)S(1)}, bf16[48,48,8]{1,2,0:T(8,128)(2,1)S(1)}, u32[]{:S(2)}, u32[]{:S(2)}) collective-permute-start(bf16[48,48,8]{1,2,0:T(8,128)(2,1)S(1)} %copy.161), channel_id=1, source_target_pairs={{0,1},{1,2},{2,3},{3,4},{4,5},{5,6},{6,7},{8,9},{9,10},{10,11},{11... | collective-permute-start | bytes 110600 | tf_op jit(solution)/shard_map/ppermute | solution.py:20
  143.8 8.9 %collective-permute-start.14 = (bf16[48,48,8]{1,2,0:T(8,128)(2,1)S(1)}, bf16[48,48,8]{1,2,0:T(8,128)(2,1)S(1)}, u32[]{:S(2)}, u32[]{:S(2)}) collective-permute-start(bf16[48,48,8]{1,2,0:T(8,128)(2,1)S(1)} %copy.157), channel_id=1, source_target_pairs={{1,0},{2,1},{3,2},{4,3},{5,4},{6,5},{7,6},{9,8},{10,9},{11,10},{12... | collective-permute-start | bytes 110600 | tf_op jit(solution)/shard_map/ppermute | solution.py:21
  157.9 1.0 copy-start.5
  158.9 38.0 %copy-start.13 = (bf16[48,32,128]{2,0,1:T(8,128)(2,1)S(1)}, bf16[48,32,128]{2,0,1:T(8,128)(2,1)}, u32[]{:S(2)}) copy-start(bf16[48,32,128]{2,0,1:T(8,128)(2,1)} %add_convert_fusion) | copy-start | bytes 1179652
